TPU v7x, 512 devices: a whole 4x8x8 slice. The times are simulated.
512 devices in a mesh: space: 16 (over z, x_hi), ens: 32 (over x_lo, y, core).
Axes of the slice: x: 4 (x_hi: 2, x_lo: 2; x = x_hi * 2 + x_lo), y: 8, z: 8, core: 2. Of those that a mesh axis runs over, the one named last changes fastest.
Arguments:
- starting_speed_field: float32 [256, 256, 2048], P('ens', 'space'), may hold values from -6 to 6
- sample_fluidity_exponent: float32 [256, 256, 2048], P('ens', 'space'), may hold values from -1.5 to 0.5
- observed: float32 [4096], P('space'), may hold values from -6 to 6
- obs_noise: float32 [256, 4096], P('ens', 'space'), may hold values from -3 to 3
- obs_var: float32 [4096], P('space'), may hold values from 0.5 to 4
- probe_cells: int32 [4096], P('space'), may hold values from 0 to 32767
- pair_cells: int32 [16, 32], P('space'), may hold values from 0 to 255
- pair_probes: int32 [16, 32], P('space'), may hold values from 0 to 5, as said below
- pair_taper: int32 [16, 32], P('space'), may hold values from 1 to 256
- pair_counts: int32 [16], P('space'), may hold values from 8 to 32, as said below
- probe_taper: int32 [16, 2, 6], P('space'), may hold values from 1 to 256
Outputs:
- prior_speed_prediction: float32 [256, 256, 2048], P('ens', 'space')
- posterior_fluidity_exponent: float32 [256, 256, 2048], P('ens', 'space')
- weighted_innovation_matrix: float32 [256, 4096], P('ens', 'space')
Inputs may be any that keep to these rules, and one draw needn't show every extreme that they name: `pair_probes`: each pair slot names a probe block of the slab or of a neighbour slab, never one outside the channel: slab 0 uses 2 to 5 and the last slab 0 to 3. `pair_counts`: slots at or beyond a slab's count are padding; some slab has all 32 slots live.
All inputs are finite; a program needn't handle non-finite values.
Results may differ from a plain program's by a relative error of at most 0.000096.
Values sent between devices are 32-bit elements; how exact they have to be, the bound alone decides.
A program may use at most 64 MiB of HBM per device.

v0:
```python
import jax
import jax.numpy as jnp
from jax import lax
from jax.sharding import PartitionSpec as P

BLK = 128
NZ = 64
STEPS = 2


DT_STEP = 0.08


def with_halo(array, sides, width):
    for axis, dim in sides:
        size, length = (lax.axis_size(axis), array.shape[dim])
        up = [(i, (i + 1) % size) for i in range(size - 1)]
        down = [(j, i) for i, j in up]
        last = lax.slice_in_dim(array, length - width, length, axis=dim)
        first = lax.slice_in_dim(array, 0, width, axis=dim)
        before = lax.ppermute(last, axis, up)
        after = lax.ppermute(first, axis, down)
        array = jnp.concatenate([before, array, after], axis=dim)
    return array


def advance(padded_u, padded_t):
    inner_u = padded_u[:, 1:-1]
    inner_t = padded_t[:, 1:-1]
    viscous = jnp.exp(inner_t)
    viscosity_halo_padding = jnp.exp(padded_t)
    running = 0.5 * (viscous + viscosity_halo_padding[:, 2:]) * (padded_u[:, 2:] - inner_u)
    running = running + 0.5 * (viscous + viscosity_halo_padding[:, :-2]) * (
        padded_u[:, :-2] - inner_u
    )
    for offset in (NZ, -NZ):
        running = running + 0.5 * (viscous + jnp.roll(viscous, offset, axis=2)) * (
            jnp.roll(inner_u, offset, axis=2) - inner_u
        )
    height = lax.broadcasted_iota(jnp.int32, inner_u.shape, 2) % NZ
    for offset, wall_cell in ((1, 0), (-1, NZ - 1)):
        at_wall = height == wall_cell
        beside_u = jnp.where(at_wall, 0.0, jnp.roll(inner_u, offset, axis=2))
        beside_v = jnp.where(at_wall, 1.0, jnp.roll(viscous, offset, axis=2))
        running = running + 0.5 * (viscous + beside_v) * (beside_u - inner_u)
    return inner_u + DT_STEP * running


def shards(
    starting_speed_field,
    sample_fluidity_exponent,
    observed,
    obs_noise,
    obs_var,
    probe_cells,
    pair_cells,
    pair_probes,
    pair_taper,
    pair_counts,
    probe_taper,
):
    highest = lax.Precision.HIGHEST
    local_members = starting_speed_field.shape[0]
    visc_padded = with_halo(sample_fluidity_exponent, (("space", 1),), 1)
    current = starting_speed_field
    for repeat in range(STEPS):
        padded_u = with_halo(current, (("space", 1),), 1)
        current = advance(padded_u, visc_padded)
    raveled_speed_field = current.reshape(local_members, -1)
    predicted = jnp.take(raveled_speed_field, probe_cells, axis=1)
    members = local_members * lax.axis_size("ens")
    mean_pred = lax.psum(jnp.sum(predicted, axis=0), "ens") / members
    anomaly = predicted - mean_pred
    scaled = (observed + obs_noise - predicted) / obs_var
    extended = with_halo(jnp.stack([anomaly, scaled]), (("space", 2),), anomaly.shape[1])
    groups = extended.shape[2] // BLK
    own_count = groups // 3
    anom_blocks = extended[0].reshape(local_members, groups, BLK)
    scaled_blocks = extended[1].reshape(local_members, groups, BLK)
    own_anom = anom_blocks[:, own_count : 2 * own_count]
    theta_blocks = sample_fluidity_exponent.reshape(local_members, -1, BLK)
    which_cells = pair_cells[0]
    which_probes = pair_probes[0]
    theta_pick = jnp.take(theta_blocks, which_cells, axis=1)
    anom_pick = jnp.take(anom_blocks, which_probes, axis=1)
    cross_part = jnp.einsum("mkr,mkq->krq", theta_pick, anom_pick, precision=highest)
    probe_part = jnp.einsum("mip,mjq->ijpq", own_anom, anom_blocks, precision=highest)
    probe_scale = probe_taper[0].astype(jnp.float32) / 256.0 / (members - 1)
    slot_live = jnp.arange(which_cells.shape[0], dtype=jnp.int32) < pair_counts[0]
    pair_scale = jnp.where(slot_live, pair_taper[0].astype(jnp.float32) / 256.0, 0.0) / (
        members - 1
    )
    cross_full, probe_full = lax.psum((cross_part, probe_part), "ens")
    weighted = probe_full * probe_scale[:, :, None, None]
    correction = jnp.einsum("ijpq,mjq->mip", weighted, scaled_blocks, precision=highest)
    gain_blocks = (
        scaled_blocks[:, own_count : 2 * own_count]
        - correction / obs_var.reshape(own_count, BLK)[None]
    )
    weighted_innovation_matrix = gain_blocks.reshape(local_members, -1)
    gain_wide = with_halo(
        weighted_innovation_matrix, (("space", 1),), weighted_innovation_matrix.shape[1]
    ).reshape(local_members, groups, BLK)
    gain_pick = jnp.take(gain_wide, which_probes, axis=1)
    updates = (
        jnp.einsum("krq,mkq->mkr", cross_full, gain_pick, precision=highest)
        * pair_scale[None, :, None]
    )
    one_hot = (
        which_cells[:, None] == jnp.arange(theta_blocks.shape[1], dtype=jnp.int32)[None, :]
    ).astype(jnp.float32)
    increment = jnp.einsum("kc,mkr->mcr", one_hot, updates, precision=highest)
    posterior_fluidity_exponent = sample_fluidity_exponent + increment.reshape(
        sample_fluidity_exponent.shape
    )
    return (current, posterior_fluidity_exponent, weighted_innovation_matrix)


def solution(mesh):
    return jax.shard_map(
        shards,
        mesh=mesh,
        in_specs=(
            P("ens", "space", None),
            P("ens", "space", None),
            P("space"),
            P("ens", "space"),
            P("space"),
            P("space"),
            P("space", None),
            P("space", None),
            P("space", None),
            P("space"),
            P("space", None, None),
        ),
        out_specs=(P("ens", "space", None), P("ens", "space", None), P("ens", "space")),
        check_vma=False,
    )
```

profile of v0, /device:TPU:198, one launch (start us, length us, event | category | flops | bytes accessed | tf_op | source)
XLA Modules:
  0.0 403.6 jit_solution(4454958973005843415)
XLA Ops:
  7.2 0.0 copy-start.1
  7.2 0.0 all-reduce.3.cloned.1.call-start
  7.2 1.4 fusion.95
  8.6 6.3 %collective-permute-start = (f32[8,1,2048]{2,1,0:T(1,128)S(1)}, f32[8,1,2048]{2,1,0:T(1,128)S(1)}, u32[]{:S(2)}, u32[]{:S(2)}) collective-permute-start(f32[8,1,2048]{2,1,0:T(1,128)S(1)} %get-tuple-element.24), channel_id=1, source_target_pairs={{0,32},{32,64},{64,96},{96,128},{128,160},{160,192},{192,224},{224... | collective-permute-start | bytes 196616 | tf_op jit(solution)/shard_map/ppermute | solution.py:21
  14.9 1.9 collective-permute-start.1
  16.9 1.3 fusion.100
  18.2 3.3 collective-permute-start.2
  21.5 6.2 %collective-permute-start.3 = (f32[8,1,2048]{2,1,0:T(1,128)S(1)}, f32[8,1,2048]{2,1,0:T(1,128)S(1)}, u32[]{:S(2)}, u32[]{:S(2)}) collective-permute-start(f32[8,1,2048]{2,1,0:T(1,128)S(1)} %get-tuple-element.35), channel_id=1, source_target_pairs={{0,32},{32,64},{64,96},{96,128},{128,160},{160,192},{192,224},{224... | collective-permute-start | bytes 196616 | tf_op jit(solution)/shard_map/ppermute | solution.py:21
  27.6 1.4 exp.8
  29.0 0.7 fusion.91
  29.8 0.0 copy-start.7
  29.8 0.0 copy-start.10
  29.8 0.0 copy-start.9
  29.8 0.7 fusion.94
  30.6 0.0 copy-start
  30.6 0.1 fusion.92
  30.7 0.1 fusion.93
  30.9 0.0 collective-permute-done
  30.9 0.0 collective-permute-done.1
  31.0 0.8 copy-done
  31.8 0.3 maximum_exponential_fusion
  32.1 0.0 collective-permute-done.2
  32.1 2.5 fusion.14
  34.6 0.4 fusion.88
  35.0 0.4 fusion.86
  35.3 0.1 fusion.90
  35.4 0.1 fusion.89
  35.5 1.9 collective-permute-start.4
  37.4 7.5 %collective-permute-start.5 = (f32[8,1,2048]{2,1,0:T(1,128)S(1)}, f32[8,1,2048]{2,1,0:T(1,128)S(1)}, u32[]{:S(2)}, u32[]{:S(2)}) collective-permute-start(f32[8,1,2048]{2,1,0:T(1,128)S(1)} %get-tuple-element.15), channel_id=1, source_target_pairs={{0,32},{32,64},{64,96},{96,128},{128,160},{160,192},{192,224},{224... | collective-permute-start | bytes 196616 | tf_op jit(solution)/shard_map/ppermute | solution.py:21
  45.0 0.1 fusion.87
  45.1 0.3 collective-permute-done.4
  45.4 1.5 collective-permute-done.5
  46.9 2.4 fusion.19
  49.3 0.0 copy-start.2
  49.3 0.0 copy-start.4
  49.3 0.0 copy-start.5
  49.3 0.0 copy-start.6
  49.3 8.5 %copy.48 = f32[8,16,2048]{0,2,1:T(8,128)} copy(f32[8,16,2048]{2,1,0:T(8,128)S(1)} %fusion.19) | data formatting | bytes 2097152 | tf_op jit(solution)/shard_map/add | solution.py:46
  57.8 6.5 %gather_fusion = f32[256,8]{1,0:T(8,128)S(1)} fusion(f32[8,32768]{0,1:T(8,128)} %bitcast.79, s32[1024]{0:T(1024)S(1)} %pad_clamp_fusion.2), kind=kCustom, calls=%fused_computation.2 | custom fusion | bytes 17408 | tf_op jit(solution)/shard_map/jit(_take)/gather | solution.py:70
  64.3 0.1 copy.49
  64.4 53.3 %psum.21 = f32[256]{0:T(256)S(1)} all-reduce(f32[256]{0:T(256)S(1)} %get-tuple-element.38), channel_id=1, replica_groups=mesh['space'=16,'ens'=32] {'ens'}, use_global_device_ids=true, to_apply=%region_1.2 | all-reduce | flops 256 | bytes 2048 | tf_op jit(solution)/shard_map/psum | solution.py:72
  117.7 8.2 %collective-permute-start.6 = (f32[2,8,256]{2,1,0:T(8,128)S(1)}, f32[2,8,256]{2,1,0:T(8,128)S(1)}, u32[]{:S(2)}, u32[]{:S(2)}) collective-permute-start(f32[2,8,256]{2,1,0:T(8,128)S(1)} %pad_maximum_fusion.6), channel_id=1, source_target_pairs={{0,32},{32,64},{64,96},{96,128},{128,160},{160,192},{192,224},{224... | collective-permute-start | bytes 49160 | tf_op jit(solution)/shard_map/ppermute | solution.py:21
  125.9 2.1 collective-permute-start.7
  128.0 0.2 reshape.150
  128.2 0.6 copy.51
  128.8 0.6 gather_fusion.1
  129.4 5.7 %collective-permute-done.7 = f32[2,8,256]{2,1,0:T(8,128)S(1)} collective-permute-done((f32[2,8,256]{2,1,0:T(8,128)S(1)}, f32[2,8,256]{2,1,0:T(8,128)S(1)}, u32[]{:S(2)}, u32[]{:S(2)}) %collective-permute-start.7) | collective-permute-done | bytes 16416 | tf_op jit(solution)/shard_map/ppermute | solution.py:22
  135.2 1.7 convolution_bitcast_fusion.1
  136.9 0.6 gather_fusion.3
  137.5 4.8 %fusion.52 = f32[32,128,128]{2,1,0:T(8,128)} fusion(f32[32,8,128]{2,1,0:T(8,128)S(1)} %gather_fusion.3, f32[32,8,128]{2,1,0:T(8,128)S(1)} %gather_fusion.1, pred[32]{0:T(512)(128)(4,1)S(1)} %compare_and_fusion, pred[32]{0:T(512)(128)(4,1)S(1)} %compare_and_fusion.1), kind=kOutput, calls=%fused_computation.75 | convolution fusion | flops 50397184 | bytes 2359360 | tf_op jit(solution)/shard_map/mkr,mkq->krq/dot_general | solution.py:86
  142.3 0.0 all-reduce.3.cloned.1.call-update
  143.0 229.4 %all-reduce.3.cloned.1.call-done = (f32[32,128,128]{2,1,0:T(8,128)}, f32[2,6,128,128]{2,3,1,0:T(8,128)}) async-done(((f32[32,128,128]{2,1,0:T(8,128)}, f32[2,6,128,128]{2,3,1,0:T(8,128)}), (f32[32,128,128]{2,1,0:T(8,128)}, f32[2,6,128,128]{2,3,1,0:T(8,128)})) %all-reduce.3.cloned.1.call-update) | async-done | bytes 2883600 | tf_op jit(solution)/shard_map/psum | solution.py:93
  372.4 1.6 slice_subtract_fusion
  374.0 0.0 copy-start.3
  374.1 5.7 %collective-permute-start.8 = (f32[8,256]{1,0:T(8,128)S(1)}, f32[8,256]{1,0:T(8,128)S(1)}, u32[]{:S(2)}, u32[]{:S(2)}) collective-permute-start(f32[8,256]{1,0:T(8,128)S(1)} %bitcast.80), channel_id=1, source_target_pairs={{0,32},{32,64},{64,96},{96,128},{128,160},{160,192},{192,224},{224... | collective-permute-start | bytes 24584 | tf_op jit(solution)/shard_map/ppermute | solution.py:21
  379.7 1.9 collective-permute-start.9
  381.7 0.0 collective-permute-done.8
  381.7 7.2 %collective-permute-done.9 = f32[8,256]{1,0:T(8,128)S(1)} collective-permute-done((f32[8,256]{1,0:T(8,128)S(1)}, f32[8,256]{1,0:T(8,128)S(1)}, u32[]{:S(2)}, u32[]{:S(2)}) %collective-permute-start.9) | collective-permute-done | bytes 8224 | tf_op jit(solution)/shard_map/ppermute | solution.py:22
  388.9 0.6 gather_fusion.2
  389.5 5.0 %fusion = f32[8,32,128]{2,0,1:T(8,128)S(1)} fusion(f32[32,128,128]{2,1,0:T(8,128)} %get-tuple-element.4, f32[32,8,128]{2,1,0:T(8,128)S(1)} %gather_fusion.2, f32[32]{0:T(128)S(1)} %fusion.82, pred[32]{0:T(512)(128)(4,1)S(1)} %compare_and_fusion), kind=kOutput, calls=%fused_computation.10 | convolution fusion | flops 50397184 | bytes 2359456 | tf_op jit(solution)/shard_map/krq,mkq->mkr/dot_general | solution.py:106
  394.5 0.6 convolution_bitcast_fusion
  395.1 0.3 copy.53
  395.5 0.2 reshape.151
  395.6 1.1 add.158
  (35 shorter events, 0.2 us)
Async XLA Ops:
  7.2 21.8 %copy-start.1 = (f32[8,16,2048]{2,1,0:T(8,128)S(1)}, f32[8,16,2048]{2,1,0:T(8,128)}, u32[]{:S(2)}) copy-start(f32[8,16,2048]{2,1,0:T(8,128)} %param.13) | copy-start | bytes 3145732
  7.2 365.2 %all-reduce.3.cloned.1.call-start = ((), (), s32[]{:S(2)}) async-start(), calls=%async_computation | async-start | bytes 5767168 | tf_op jit(solution)/shard_map/psum | solution.py:93
  8.6 22.3 %collective-permute-start = (f32[8,1,2048]{2,1,0:T(1,128)S(1)}, f32[8,1,2048]{2,1,0:T(1,128)S(1)}, u32[]{:S(2)}, u32[]{:S(2)}) collective-permute-start(f32[8,1,2048]{2,1,0:T(1,128)S(1)} %get-tuple-element.24), channel_id=1, source_target_pairs={{0,32},{32,64},{64,96},{96,128},{128,160},{160,192},{192,224},{224... | collective-permute-start | bytes 196616 | tf_op jit(solution)/shard_map/ppermute | solution.py:21
  14.9 16.0 %collective-permute-start.1 = (f32[8,1,2048]{2,1,0:T(1,128)S(1)}, f32[8,1,2048]{2,1,0:T(1,128)S(1)}, u32[]{:S(2)}, u32[]{:S(2)}) collective-permute-start(f32[8,1,2048]{2,1,0:T(1,128)S(1)} %get-tuple-element.25), channel_id=1, source_target_pairs={{32,0},{64,32},{96,64},{128,96},{160,128},{192,160},{224,192},{256... | collective-permute-start | bytes 196616 | tf_op jit(solution)/shard_map/ppermute | solution.py:22
  18.2 14.0 %collective-permute-start.2 = (f32[8,1,2048]{2,1,0:T(1,128)S(1)}, f32[8,1,2048]{2,1,0:T(1,128)S(1)}, u32[]{:S(2)}, u32[]{:S(2)}) collective-permute-start(f32[8,1,2048]{2,1,0:T(1,128)S(1)} %get-tuple-element.34), channel_id=1, source_target_pairs={{32,0},{64,32},{96,64},{128,96},{160,128},{192,160},{224,192},{256... | collective-permute-start | bytes 196616 | tf_op jit(solution)/shard_map/ppermute | solution.py:22
  21.5 10.6 %collective-permute-start.3 = (f32[8,1,2048]{2,1,0:T(1,128)S(1)}, f32[8,1,2048]{2,1,0:T(1,128)S(1)}, u32[]{:S(2)}, u32[]{:S(2)}) collective-permute-start(f32[8,1,2048]{2,1,0:T(1,128)S(1)} %get-tuple-element.35), channel_id=1, source_target_pairs={{0,32},{32,64},{64,96},{96,128},{128,160},{160,192},{192,224},{224... | collective-permute-start | bytes 196616 | tf_op jit(solution)/shard_map/ppermute | solution.py:21
  29.8 1.0 copy-start.7
  29.8 1.0 copy-start.10
  29.8 1.1 copy-start.9
  30.6 1.2 copy-start
  35.5 9.9 %collective-permute-start.4 = (f32[8,1,2048]{2,1,0:T(1,128)S(1)}, f32[8,1,2048]{2,1,0:T(1,128)S(1)}, u32[]{:S(2)}, u32[]{:S(2)}) collective-permute-start(f32[8,1,2048]{2,1,0:T(1,128)S(1)} %get-tuple-element.14), channel_id=1, source_target_pairs={{32,0},{64,32},{96,64},{128,96},{160,128},{192,160},{224,192},{256... | collective-permute-start | bytes 196616 | tf_op jit(solution)/shard_map/ppermute | solution.py:22
  37.4 9.4 %collective-permute-start.5 = (f32[8,1,2048]{2,1,0:T(1,128)S(1)}, f32[8,1,2048]{2,1,0:T(1,128)S(1)}, u32[]{:S(2)}, u32[]{:S(2)}) collective-permute-start(f32[8,1,2048]{2,1,0:T(1,128)S(1)} %get-tuple-element.15), channel_id=1, source_target_pairs={{0,32},{32,64},{64,96},{96,128},{128,160},{160,192},{192,224},{224... | collective-permute-start | bytes 196616 | tf_op jit(solution)/shard_map/ppermute | solution.py:21
  49.3 8.5 %copy-start.2 = (f32[8,16,2048]{2,1,0:T(8,128)}, f32[8,16,2048]{2,1,0:T(8,128)S(1)}, u32[]{:S(2)}) copy-start(f32[8,16,2048]{2,1,0:T(8,128)S(1)} %fusion.19) | copy-start | bytes 3145732
  49.3 15.1 %copy-start.4 = (f32[8,256]{1,0:T(8,128)S(1)}, f32[8,256]{1,0:T(8,128)}, u32[]{:S(2)}) copy-start(f32[8,256]{1,0:T(8,128)} %param.16) | copy-start | bytes 24580
  49.3 15.1 %copy-start.5 = (f32[256]{0:T(256)S(1)}, f32[256]{0:T(256)}, u32[]{:S(2)}) copy-start(f32[256]{0:T(256)} %param.17) | copy-start | bytes 3076
  49.3 15.1 %copy-start.6 = (f32[256]{0:T(256)S(1)}, f32[256]{0:T(256)}, u32[]{:S(2)}) copy-start(f32[256]{0:T(256)} %param.15) | copy-start | bytes 3076
  117.7 11.7 %collective-permute-start.6 = (f32[2,8,256]{2,1,0:T(8,128)S(1)}, f32[2,8,256]{2,1,0:T(8,128)S(1)}, u32[]{:S(2)}, u32[]{:S(2)}) collective-permute-start(f32[2,8,256]{2,1,0:T(8,128)S(1)} %pad_maximum_fusion.6), channel_id=1, source_target_pairs={{0,32},{32,64},{64,96},{96,128},{128,160},{160,192},{192,224},{224... | collective-permute-start | bytes 49160 | tf_op jit(solution)/shard_map/ppermute | solution.py:21
  125.9 9.2 %collective-permute-start.7 = (f32[2,8,256]{2,1,0:T(8,128)S(1)}, f32[2,8,256]{2,1,0:T(8,128)S(1)}, u32[]{:S(2)}, u32[]{:S(2)}) collective-permute-start(f32[2,8,256]{2,1,0:T(8,128)S(1)} %pad_maximum_fusion.6), channel_id=1, source_target_pairs={{32,0},{64,32},{96,64},{128,96},{160,128},{192,160},{224,192},{256... | collective-permute-start | bytes 49160 | tf_op jit(solution)/shard_map/ppermute | solution.py:22
  142.3 0.7 copy-start.8
  142.3 239.3 %copy-start.11 = (s32[1,32]{1,0:T(1,128)S(1)}, s32[1,32]{1,0:T(1,128)}, u32[]{:S(2)}) copy-start(s32[1,32]{1,0:T(1,128)} %param.21) | copy-start | bytes 388
  374.0 21.1 %copy-start.3 = (f32[8,2,128]{2,0,1:T(8,128)}, f32[8,2,128]{2,0,1:T(8,128)S(1)}, u32[]{:S(2)}) copy-start(f32[8,2,128]{2,0,1:T(8,128)S(1)} %slice_subtract_fusion) | copy-start | bytes 24580
  374.1 7.6 %collective-permute-start.8 = (f32[8,256]{1,0:T(8,128)S(1)}, f32[8,256]{1,0:T(8,128)S(1)}, u32[]{:S(2)}, u32[]{:S(2)}) collective-permute-start(f32[8,256]{1,0:T(8,128)S(1)} %bitcast.80), channel_id=1, source_target_pairs={{0,32},{32,64},{64,96},{96,128},{128,160},{160,192},{192,224},{224... | collective-permute-start | bytes 24584 | tf_op jit(solution)/shard_map/ppermute | solution.py:21
  379.7 9.2 %collective-permute-start.9 = (f32[8,256]{1,0:T(8,128)S(1)}, f32[8,256]{1,0:T(8,128)S(1)}, u32[]{:S(2)}, u32[]{:S(2)}) collective-permute-start(f32[8,256]{1,0:T(8,128)S(1)} %bitcast.81), channel_id=1, source_target_pairs={{32,0},{64,32},{96,64},{128,96},{160,128},{192,160},{224,192},{256... | collective-permute-start | bytes 24584 | tf_op jit(solution)/shard_map/ppermute | solution.py:22
Sparse Core Ops, SparseCore 0:
  142.5 229.8 all-reduce.2
where the time goes:
time: 404 us
  waiting for transfers between devices  244 us (60%)
  blocking collectives  53.3 us (13%)
  starting transfers between devices  45.1 us (11%)
  local copies, waits for them, and re-layouts  25.7 us (6%)
  between operations  15.2 us (4%)
  matrix products  13.8 us (3%)
  other arithmetic  6.41 us (2%)
    psum x1, waiting for transfers between devices, shards(): cross_full, probe_full = lax.psum((cross_part, probe_part), 'ens')  229 us
    psum x1, blocking collectives, shards(): mean_pred = lax.psum(jnp.sum(predicted, axis=0), 'ens') / members  53.3 us
    ppermute x5, starting transfers between devices, with_halo(): before = lax.ppermute(last, axis, up)  33.9 us
    ppermute x5, waiting for transfers between devices, with_halo(): after = lax.ppermute(first, axis, down)  13.3 us
    ppermute x5, starting transfers between devices, with_halo(): after = lax.ppermute(first, axis, down)  11.2 us
    add x1, local copies, waits for them, and re-layouts, advance(): return inner_u + DT_STEP * running  8.49 us
  transfers between devices with their start and end apart: 11, of which 5 were waited for; matrix products, arithmetic and copies ran while one was open for 2% of the time, Pallas kernels for 0%

commit v1 on v0

v1 whole, which is shorter than its diff:
```python
import functools

import jax
import jax.numpy as jnp
from jax import lax
from jax.experimental import pallas as pl
from jax.experimental.pallas import tpu as pltpu
from jax.sharding import PartitionSpec as P

BLK = 128
NZ = 64
DT_STEP = 0.08
COEF = 0.5 * DT_STEP

NS = 16
NYR = 8
G = 4
PLANES = 16
LT = 16
MEM = 8
ALL = 256
SLOTS = 32
SPG = SLOTS // G

MESH = pl.DeviceIdType.MESH
HIGHEST = lax.Precision.HIGHEST
F32 = jnp.float32


def dot(a, b, dims):
    return lax.dot_general(a, b, (dims, ((), ())), precision=HIGHEST, preferred_element_type=F32)


NN = ((1,), (0,))
NT = ((1,), (1,))


def tile(t):
    return slice(t * BLK, (t + 1) * BLK)


def tiles(ref, *where):
    return [ref[(*where, slice(None), tile(t))] for t in range(LT)]


def put(ref, values, *where):
    for t in range(LT):
        ref[(*where, slice(None), tile(t))] = values[t]


def main_kernel(
    u_hbm, t_hbm, obs_hbm, noise_hbm, var_hbm, cells, pair_cells, pair_probes, probe_taper, *refs
):
    (
    prior_hbm, gain_out, upd_out,
    ust, tst, u0, th, vv, cx, cy, cz, cd, uh, thh, ps, pr, u1, u2, ost,
    thg, agb, anom, a_own, a_win, k_own, k_win, us, upd,
    in_sem, out_sem, halo_s, halo_r, sub_s, sub_r, ring_s, ring_r, ag1_s, ag1_r, ag2_s, ag2_r, ax_s, ax_r,
    kx_s, kx_r, ux_s, ux_r,
    obs_ref, noise_ref, var_ref, small_sem,
    ) = refs
    s = lax.axis_index("space")
    e = lax.axis_index("ens")
    xl, y, c = e // (2 * NYR), (e // 2) % NYR, e % 2
    g = xl * 2 + c
    has_up, has_dn = s < NS - 1, s > 0
    s_up, s_dn = jnp.minimum(s + 1, NS - 1), jnp.maximum(s - 1, 0)

    def ens_of(gg, yy):
        return (gg // 2) * (2 * NYR) + yy * 2 + gg % 2

    def remote(src, dst, ss, rs, space, ens):
        return pltpu.make_async_remote_copy(
            src_ref=src, dst_ref=dst, send_sem=ss, recv_sem=rs, device_id=(space, ens), device_id_type=MESH
        )

    sub_g = [(g + d) % G for d in range(1, G)]

    loads = []
    for t in range(LT):
        for k, (src, dst) in enumerate(((t_hbm, tst), (u_hbm, ust))):
            loads.append(pltpu.make_async_copy(src.at[:, tile(t)], dst.at[t], in_sem.at[k * LT + t]))
    for copy in loads:
        copy.start()
    small_src = (obs_hbm, noise_hbm, var_hbm)
    small_dst = (obs_ref, noise_ref, var_ref)
    smalls = [pltpu.make_async_copy(a, b, small_sem.at[i]) for i, (a, b) in enumerate(zip(small_src, small_dst))]
    for copy in smalls:
        copy.start()

    bar = pltpu.get_barrier_semaphore()
    for d in range(1, NYR):
        pl.semaphore_signal(bar, 1, device_id=(s, ens_of(g, (y + d) % NYR)), device_id_type=MESH)
    for gg in sub_g:
        pl.semaphore_signal(bar, 1, device_id=(s, ens_of(gg, y)), device_id_type=MESH)

    @pl.when(has_up)
    def _():
        for gg in range(G):
            pl.semaphore_signal(bar, 1, device_id=(s_up, ens_of(gg, y)), device_id_type=MESH)

    @pl.when(has_dn)
    def _():
        for gg in range(G):
            pl.semaphore_signal(bar, 1, device_id=(s_dn, ens_of(gg, y)), device_id_type=MESH)

    lane = lax.broadcasted_iota(jnp.int32, (MEM, BLK), 1)
    low = lane < NZ
    height = lane % NZ
    top = height == NZ - 1
    wall = (height == 0) | top

    def y_up(x):
        r = [pltpu.roll(v, NZ, 1) for v in x]
        return [jnp.where(low, r[t], r[(t + 1) % LT]) for t in range(LT)]

    def y_down(x):
        r = [pltpu.roll(v, NZ, 1) for v in x]
        return [jnp.where(low, r[t - 1], r[t]) for t in range(LT)]

    def bring(p):
        for t in range(LT):
            rows = pl.ds(p, MEM, PLANES)
            th[p * LT + t] = tst[t, rows, :]
            u0[p, :, tile(t)] = ust[t, rows, :]

    def viscosity(p):
        for t in range(LT):
            vv[p, :, tile(t)] = jnp.exp(th[p * LT + t])

    def loop(lo, hi, fn):
        def body(p, carry):
            fn(p)
            return carry

        lax.fori_loop(lo, hi, body, 0)

    def coefficients(p):
        v = tiles(vv, p)
        vy = y_up(v)
        for t in range(LT):
            cy[p, :, tile(t)] = COEF * (v[t] + vy[t])
            cz[p, :, tile(t)] = jnp.where(top, 0.0, COEF * (v[t] + pltpu.roll(v[t], BLK - 1, 1)))
            cd[p, :, tile(t)] = 1.0 - jnp.where(wall, COEF * (v[t] + 1.0), 0.0)

    def face(p):
        for t in range(LT):
            cx[p, :, tile(t)] = COEF * (vv[p - 1, :, tile(t)] + vv[p, :, tile(t)])

    def partial(src, off, p, lower, upper):
        u = tiles(src, p + off)
        uy = y_up(u)
        fy = [cy[p, :, tile(t)] * (uy[t] - u[t]) for t in range(LT)]
        fd = y_down(fy)
        out = []
        for t in range(LT):
            fz = cz[p, :, tile(t)] * (pltpu.roll(u[t], BLK - 1, 1) - u[t])
            new = cd[p, :, tile(t)] * u[t] + ((fy[t] - fd[t]) + (fz - pltpu.roll(fz, 1, 1)))
            if upper:
                new = new + cx[p + 1, :, tile(t)] * (src[p + 1 + off, :, tile(t)] - u[t])
            if lower:
                new = new - cx[p, :, tile(t)] * (u[t] - src[p - 1 + off, :, tile(t)])
            out.append(new)
        return out

    for copy in loads:
        copy.wait()
    for copy in smalls:
        copy.wait()

    for p in (0, PLANES - 1):
        bring(p)

    pl.semaphore_wait(bar, NYR - 1 + G - 1 + G * has_up.astype(jnp.int32) + G * has_dn.astype(jnp.int32))

    ends = ((0, PLANES - 1, s_up, has_up), (1, 0, s_dn, has_dn))
    halo_field = [
        [
            remote(th.at[pl.ds(p * LT, LT)], thh.at[d], halo_s.at[d * 3], halo_r.at[d * 3], dest, e),
            remote(u0.at[p], uh.at[d], halo_s.at[d * 3 + 1], halo_r.at[d * 3 + 1], dest, e),
        ]
        for d, p, dest, _ in ends
    ]
    halo_part = [
        remote(ps.at[d], pr.at[d], halo_s.at[d * 3 + 2], halo_r.at[d * 3 + 2], dest, e) for d, p, dest, _ in ends
    ]
    for d, p, dest, has in ends:

        @pl.when(has)
        def _(d=d):
            for copy in halo_field[d]:
                copy.start()

    def pick(k, carry):
        upd[k] = th[pair_cells[0, k]]
        return carry

    loop(1, PLANES - 1, bring)
    lax.fori_loop(0, SLOTS, pick, 0, unroll=4)
    sub_copies = []
    for d, gg in enumerate(sub_g):
        sub_copies.append(
            remote(upd.at[pl.ds(gg * SPG, SPG)], thg.at[:, y, g], sub_s.at[d], sub_r.at[d], s, ens_of(gg, y))
        )
    for copy in sub_copies:
        copy.start()
    for i in range(SPG):
        thg[i, y, g] = upd[g * SPG + i]

    for p in (0, 1, PLANES - 2, PLANES - 1):
        viscosity(p)
    for p in (0, PLANES - 1):
        coefficients(p)
    face(1)
    face(PLANES - 1)
    put(ps, partial(u0, 0, PLANES - 1, True, False), 0)
    put(ps, partial(u0, 0, 0, False, True), 1)
    for d, p, dest, has in ends:

        @pl.when(has)
        def _(d=d):
            halo_part[d].start()

    right, left = ens_of(g, (y + 1) % NYR), ens_of(g, (y + NYR - 1) % NYR)
    half = SPG // 2

    def ring(step):
        a, b = (y + NYR - step) % NYR, (y + step) % NYR
        if step < 3:
            src_r, src_l = thg.at[:, a], thg.at[:, b]
        else:
            src_r, src_l = thg.at[pl.ds(0, half), a], thg.at[pl.ds(half, half), b]
        return [
            remote(src_r, src_r, ring_s.at[step * 2], ring_r.at[step * 2], s, right),
            remote(src_l, src_l, ring_s.at[step * 2 + 1], ring_r.at[step * 2 + 1], s, left),
        ]

    rings = [ring(step) for step in range(4)]

    loop(2, PLANES - 2, viscosity)
    for copy in sub_copies:
        copy.wait_recv()
    for copy in rings[0]:
        copy.start()
    loop(1, PLANES - 1, coefficients)
    loop(2, PLANES - 1, face)

    def first(p):
        put(u1, partial(u0, 0, p, True, True), p + 1)

    def second(p):
        for t, value in enumerate(partial(u1, 1, p, True, True)):
            u2[p * LT + t] = value

    loop(1, PLANES - 1, first)
    loop(2, PLANES - 2, second)
    for copy in rings[0]:
        copy.wait_recv()
    for copy in rings[1]:
        copy.start()

    for d, p, dest, has in ends:

        @pl.when(jnp.logical_not((has_dn, has_up)[d]))
        def _(d=d):
            uh[d] = jnp.zeros_like(uh[d])
            thh[d] = jnp.zeros_like(thh[d])
            pr[d] = jnp.zeros_like(pr[d])

    for d, p, dest, has in ends:

        @pl.when((has_dn, has_up)[d])
        def _(d=d):
            for copy in halo_field[d]:
                copy.wait_recv()
            halo_part[d].wait_recv()

    keep_dn = has_dn.astype(F32)
    keep_up = has_up.astype(F32)
    for t in range(LT):
        w = (slice(None), tile(t))
        face_lo = COEF * (jnp.exp(thh[0, t]) + vv[(0, *w)])
        flux = face_lo * (u0[(0, *w)] - uh[(0, *w)])
        cx[(0, *w)] = face_lo
        u1[(0, *w)] = (pr[(0, *w)] + flux) * keep_dn
        u1[(1, *w)] = ps[(1, *w)] - flux
        face_hi = COEF * (jnp.exp(thh[1, t]) + vv[(PLANES - 1, *w)])
        flux = face_hi * (uh[(1, *w)] - u0[(PLANES - 1, *w)])
        cx[(PLANES, *w)] = face_hi
        u1[(PLANES + 1, *w)] = (pr[(1, *w)] - flux) * keep_up
        u1[(PLANES, *w)] = ps[(0, *w)] + flux
    loop(0, 2, second)
    loop(PLANES - 2, PLANES, second)

    def probe(i, accs):
        new = []
        for b in range(2):
            cell = cells[b * BLK + i]
            row = u2[cell >> 7]
            one = jnp.sum(jnp.where(lane == (cell & (BLK - 1)), row, 0.0), axis=1, keepdims=True)
            new.append(jnp.where(lane == i, one, accs[b]))
        return tuple(new)

    zero = jnp.zeros((MEM, BLK), F32)
    pred = lax.fori_loop(0, BLK, probe, (zero, zero), unroll=4)
    for b in range(2):
        agb[y, g, :, tile(b)] = pred[b]

    order = [4, 3, 5, 2, 6, 1, 7]
    ag1 = [
        remote(agb.at[y, g], agb.at[y, g], ag1_s.at[d - 1], ag1_r.at[d - 1], s, ens_of(g, (y + d) % NYR)) for d in order
    ]
    for copy in ag1:
        copy.start()
    for copy in rings[1]:
        copy.wait_recv()
    for copy in rings[2]:
        copy.start()

    def back(p):
        for t in range(LT):
            ost[t, pl.ds(p, MEM, PLANES), :] = u2[p * LT + t]

    loop(0, PLANES, back)
    stores = [pltpu.make_async_copy(ost.at[t], prior_hbm.at[:, tile(t)], out_sem.at[t]) for t in range(LT)]
    for copy in stores:
        copy.start()
    scaled = [
        (obs_ref[:, tile(b)] + noise_ref[:, tile(b)] - pred[b]) / var_ref[:, tile(b)] for b in range(2)
    ]
    for copy in ag1:
        copy.wait_recv()
    ag2 = [
        remote(agb.at[:, g], agb.at[:, g], ag2_s.at[d], ag2_r.at[d], s, ens_of(gg, y)) for d, gg in enumerate(sub_g)
    ]
    for copy in ag2:
        copy.start()
    for copy in ag2:
        copy.wait_recv()

    everyone = agb[...].reshape(ALL, 2 * BLK)
    anom[...] = everyone - jnp.sum(everyone, axis=0, keepdims=True) * (1.0 / ALL)
    for b in range(2):
        part = dot(scaled[b], anom[:, tile(b)], NT)
        a_own[b] = part
        a_win[2 + b] = part
    ax = [
        remote(a_own, a_win.at[pl.ds(0, 2)], ax_s.at[0], ax_r.at[0], s_up, e),
        remote(a_own, a_win.at[pl.ds(4, 2)], ax_s.at[1], ax_r.at[1], s_dn, e),
    ]
    for d, has in ((0, has_up), (1, has_dn)):

        @pl.when(has)
        def _(d=d):
            ax[d].start()

    for copy in rings[2]:
        copy.wait_recv()
    for copy in rings[3]:
        copy.start()

    for d, has in ((0, has_dn), (1, has_up)):

        @pl.when(jnp.logical_not(has))
        def _(d=d):
            for b in range(2):
                a_win[4 * d + b] = jnp.zeros((MEM, ALL), F32)
                k_win[4 * d + b] = jnp.zeros((G, MEM, ALL), F32)

        @pl.when(has)
        def _(d=d):
            ax[d].wait_recv()

    for b in range(2):
        mix = probe_taper[0, b, 0].astype(F32) * a_win[0]
        for j in range(1, 6):
            mix = mix + probe_taper[0, b, j].astype(F32) * a_win[j]
        corr = dot(mix * (1.0 / 256.0 / (ALL - 1)), anom[:, tile(b)], NN)
        gain = scaled[b] - corr / var_ref[:, tile(b)]
        gain_out[:, tile(b)] = gain
        kk = dot(gain, anom[:, tile(b)], NT)
        k_own[b] = kk
        k_win[2 + b, g] = kk
    kx_up = [remote(k_own, k_win.at[pl.ds(0, 2), g], kx_s.at[gg], kx_r.at[g], s_up, ens_of(gg, y)) for gg in range(G)]
    kx_dn = [
        remote(k_own, k_win.at[pl.ds(4, 2), g], kx_s.at[G + gg], kx_r.at[G + g], s_dn, ens_of(gg, y))
        for gg in range(G)
    ]
    kx_own = [
        remote(k_own, k_win.at[pl.ds(2, 2), g], kx_s.at[2 * G + d], kx_r.at[2 * G + d], s, ens_of(gg, y))
        for d, gg in enumerate(sub_g)
    ]

    @pl.when(has_up)
    def _():
        for copy in kx_up:
            copy.start()

    @pl.when(has_dn)
    def _():
        for copy in kx_dn:
            copy.start()

    for copy in kx_own:
        copy.start()
    for copy in rings[3]:
        copy.wait_recv()
    for copy in kx_own:
        copy.wait_recv()
    for base, has in ((0, has_dn), (G, has_up)):

        @pl.when(has)
        def _(base=base):
            for gg in range(G):
                remote(
                    k_own, k_win.at[pl.ds(0, 2), g], kx_s.at[0], kx_r.at[base + gg], s, ens_of(gg, y)
                ).wait_recv()

    for i in range(SPG):
        k = g * SPG + i
        left_side = k_win[pair_probes[0, k]].reshape(G * MEM, ALL)
        us[i] = dot(left_side, thg[i].reshape(ALL, BLK), NN).reshape(G, MEM, BLK)
    for copy in sub_copies:
        copy.wait_send()
    ux = [
        remote(us.at[:, gg], upd_out.at[pl.ds(g * SPG, SPG)], ux_s.at[d], ux_r.at[d], s, ens_of(gg, y))
        for d, gg in enumerate(sub_g)
    ]
    for copy in ux:
        copy.start()
    for i in range(SPG):
        upd_out[g * SPG + i] = us[i, g]

    for d, p, dest, has in ends:

        @pl.when(has)
        def _(d=d):
            for copy in halo_field[d]:
                copy.wait_send()
            halo_part[d].wait_send()
            ax[d].wait_send()
            for copy in (kx_up, kx_dn)[d]:
                copy.wait_send()

    for copy in [q for step in rings for q in step] + ag1 + ag2 + kx_own:
        copy.wait_send()
    for copy in stores:
        copy.wait()
    for copy in ux:
        copy.wait()


def tail_kernel(pair_cells, pair_taper, pair_counts, t_hbm, upd, post_out, st, sem_i, sem_o):
    loads = [pltpu.make_async_copy(t_hbm.at[:, tile(t)], st.at[t], sem_i.at[t]) for t in range(LT)]
    for copy in loads:
        copy.start()
    for copy in loads:
        copy.wait()

    def add(k, carry):
        b = pair_cells[0, k]
        w = jnp.where(k < pair_counts[0], pair_taper[0, k].astype(F32) * (1.0 / 256.0), 0.0) * (1.0 / (ALL - 1))
        rows = pl.ds(b // LT, MEM, PLANES)
        st[b % LT, rows, :] = st[b % LT, rows, :] + w * upd[k]
        return carry

    lax.fori_loop(0, SLOTS, add, 0)
    stores = [pltpu.make_async_copy(st.at[t], post_out.at[:, tile(t)], sem_o.at[t]) for t in range(LT)]
    for copy in stores:
        copy.start()
    for copy in stores:
        copy.wait()


def shards(u, theta, observed, obs_noise, obs_var, probe_cells, pair_cells, pair_probes, pair_taper, pair_counts, probe_taper):
    shape = u.shape
    rows, cols = shape[0] * shape[1], shape[2]
    u, theta = u.reshape(rows, cols), theta.reshape(rows, cols)
    any_ = pl.BlockSpec(memory_space=pl.ANY)
    vmem = pl.BlockSpec(memory_space=pltpu.VMEM)
    smem = pl.BlockSpec(memory_space=pltpu.SMEM)
    big = (PLANES, MEM, cols)
    dma = pltpu.SemaphoreType.DMA

    def buf(*dims):
        return pltpu.VMEM(dims, F32)

    prior, gain, upd = pl.pallas_call(
        main_kernel,
        name="assimilate",
        out_shape=(
            jax.ShapeDtypeStruct((rows, cols), F32),
            jax.ShapeDtypeStruct((MEM, 2 * BLK), F32),
            jax.ShapeDtypeStruct((SLOTS, MEM, BLK), F32),
        ),
        in_specs=[any_] * 5 + [smem] * 4,
        out_specs=(any_, vmem, vmem),
        scratch_shapes=[
            buf(LT, rows, BLK), buf(LT, rows, BLK), buf(*big), buf(PLANES * LT, MEM, BLK), buf(*big),
            buf(PLANES + 1, MEM, cols), buf(*big), buf(*big), buf(*big),
            buf(2, MEM, cols), buf(2, LT, MEM, BLK), buf(2, MEM, cols), buf(2, MEM, cols),
            buf(PLANES + 2, MEM, cols), buf(PLANES * LT, MEM, BLK), buf(LT, rows, BLK),
            buf(SPG, NYR, G, MEM, BLK), buf(NYR, G, MEM, 2 * BLK), buf(ALL, 2 * BLK),
            buf(2, MEM, ALL), buf(6, MEM, ALL), buf(2, MEM, ALL), buf(6, G, MEM, ALL),
            buf(SPG, G, MEM, BLK), buf(SLOTS, MEM, BLK),
            dma((2 * LT,)), dma((LT,)), dma((6,)), dma((6,)), dma((3,)), dma((3,)), dma((8,)), dma((8,)),
            dma((7,)), dma((7,)), dma((3,)), dma((3,)), dma((2,)), dma((2,)),
            dma((11,)), dma((11,)), dma((3,)), dma((3,)),
            buf(1, 2 * BLK), buf(MEM, 2 * BLK), buf(1, 2 * BLK), dma((3,)),
        ],
        compiler_params=pltpu.CompilerParams(
            collective_id=0, has_side_effects=True
        ),
    )(
        u, theta, observed.reshape(1, -1), obs_noise, obs_var.reshape(1, -1), probe_cells, pair_cells, pair_probes,
        probe_taper,
    )
    post = pl.pallas_call(
        tail_kernel,
        name="tail",
        out_shape=jax.ShapeDtypeStruct((rows, cols), F32),
        in_specs=[smem, smem, smem, any_, vmem],
        out_specs=any_,
        scratch_shapes=[buf(LT, rows, BLK), dma((LT,)), dma((LT,))],
    )(pair_cells, pair_taper, pair_counts, theta, upd)
    return prior.reshape(shape), post.reshape(shape), gain


def solution(mesh):
    return jax.shard_map(
        shards,
        mesh=mesh,
        in_specs=(
            P("ens", "space", None), P("ens", "space", None), P("space"), P("ens", "space"), P("space"), P("space"),
            P("space", None), P("space", None), P("space", None), P("space"), P("space", None, None),
        ),
        out_specs=(P("ens", "space", None), P("ens", "space", None), P("ens", "space")),
        check_vma=False,
    )
```

time: 404 us -> 60.2 us (0.15)
  the two profiles are of different devices: /device:TPU:198 before, /device:TPU:197 now
where the time goes in v1:
time: 60.2 us; the launch traced here: 59.9 us
  Pallas kernels  57 us (95%)
  local copies, waits for them, and re-layouts  1.58 us (3%)
  between operations  1.32 us (2%)
    pallas_call x1, Pallas kernels, shards(): pl.pallas_call(main_kernel, name='assimilate', out_shape=(jax.ShapeDtypeS...  53 us
    pallas_call x1, Pallas kernels, shards(): pl.pallas_call(tail_kernel, name='tail', out_shape=jax.ShapeDtypeStruct((...  4.04 us
    unnamed x6, local copies, waits for them, and re-layouts  1.58 us

profile of v1, /device:TPU:197, one launch (start us, length us, event | category | flops | bytes accessed | tf_op | source)
XLA Modules:
  0.0 59.9 jit_solution(3156947762371479208)
XLA Ops:
  1.3 53.0 %assimilate.1 = (f32[128,2048]{1,0:T(8,128)}, f32[8,256]{1,0:T(8,128)}, f32[32,8,128]{2,1,0:T(8,128)}) custom-call(f32[128,2048]{1,0:T(8,128)} %bitcast.10, f32[128,2048]{1,0:T(8,128)} %bitcast.6, f32[1,256]{1,0:T(1,128)} %bitcast.11, f32[8,256]{1,0:T(8,128)} %noise_hbm.1, f32[1,256]{1,0:T(1,128)} %bitcast.12, s32[256]{0:T(256)} %cells.1, ...), custom_call_target="tpu_custom_call" | custom-call | tf_op jit(solution)/shard_map/assimilate/pallas_call | solution.py:488
  54.3 0.0 copy-start
  54.3 4.0 %tail.1 = f32[128,2048]{1,0:T(8,128)} custom-call(s32[1,32]{1,0:T(1,128)} %pair_cells.3, s32[1,32]{1,0:T(1,128)} %pair_taper.1, s32[1]{0:T(128)S(6)} %copy.16.pair_counts, f32[128,2048]{1,0:T(8,128)} %bitcast.7, f32[32,8,128]{2,1,0:T(8,128)} %get-tuple-element.7.upd), custom_call_target="tpu_custom_call" | custom-call | tf_op jit(solution)/shard_map/tail/pallas_call | solution.py:518
  58.3 0.0 copy-done
  58.3 0.0 copy-start.1
  58.3 1.0 %copy.17 = f32[8,16,2048]{2,1,0:T(8,128)} copy(f32[8,16,2048]{2,1,0:T(8,128)S(1)} %bitcast.9) | data formatting | bytes 2097152
  59.3 0.0 copy-done.1
  59.3 0.6 copy.18
Async XLA Ops:
  54.3 4.1 %copy-start = (f32[128,2048]{1,0:T(8,128)S(1)}, f32[128,2048]{1,0:T(8,128)}, u32[]{:S(2)}) copy-start(f32[128,2048]{1,0:T(8,128)} %get-tuple-element.6) | copy-start | bytes 3145732
  58.3 1.0 %copy-start.1 = (f32[8,256]{1,0:T(8,128)S(1)}, f32[8,256]{1,0:T(8,128)}, u32[]{:S(2)}) copy-start(f32[8,256]{1,0:T(8,128)} %get-tuple-element.14) | copy-start | bytes 24580

commit v2 on v1

v2 whole, which is shorter than its diff:
```python
import functools

import jax
import jax.numpy as jnp
from jax import lax
from jax.experimental import pallas as pl
from jax.experimental.pallas import tpu as pltpu
from jax.sharding import PartitionSpec as P

BLK = 128
NZ = 64
DT_STEP = 0.08
COEF = 0.5 * DT_STEP

NS = 16
NYR = 8
G = 4
PLANES = 16
LT = 16
MEM = 8
ALL = 256
SLOTS = 32
SPG = SLOTS // G

MESH = pl.DeviceIdType.MESH
HIGHEST = lax.Precision.HIGHEST
F32 = jnp.float32


def dot(a, b, dims):
    return lax.dot_general(a, b, (dims, ((), ())), precision=HIGHEST, preferred_element_type=F32)


NN = ((1,), (0,))
NT = ((1,), (1,))


def tile(t):
    return slice(t * BLK, (t + 1) * BLK)


def tiles(ref, *where):
    return [ref[(*where, slice(None), tile(t))] for t in range(LT)]


def put(ref, values, *where):
    for t in range(LT):
        ref[(*where, slice(None), tile(t))] = values[t]


def main_kernel(
    u_hbm, t_hbm, *refs
):
    smalls_hbm, refs = refs[:7], refs[7:]
    (
        ost, tst, gain_out, upd_out,
        ust, u0, th, vv, cx, cy, cz, cd, uh, thh, ps, pr, u1, u2,
        thg, agb, scw, anom, a_part, a_win, k_own, k_win, us, upd,
        obs_ref, noise_ref, var_ref, cells, pair_cells, pair_probes, probe_taper,
        in_sem, small_sem, halo_s, halo_r, sub_s, sub_r, ring_s, ring_r, ag1_s, ag1_r, ag2_s, ag2_r, sc_s, sc_r,
        ax_s, ax_r, kx_s, kx_r, ux_s, ux_r,
    ) = refs
    s = lax.axis_index("space")
    e = lax.axis_index("ens")
    xl, y, c = e // (2 * NYR), (e // 2) % NYR, e % 2
    g = xl * 2 + c
    has_up, has_dn = s < NS - 1, s > 0
    s_up, s_dn = jnp.minimum(s + 1, NS - 1), jnp.maximum(s - 1, 0)

    def ens_of(gg, yy):
        return (gg // 2) * (2 * NYR) + yy * 2 + gg % 2

    def remote(src, dst, ss, rs, space, ens):
        return pltpu.make_async_remote_copy(
            src_ref=src, dst_ref=dst, send_sem=ss, recv_sem=rs, device_id=(space, ens), device_id_type=MESH
        )

    sub_g = [(g + d) % G for d in range(1, G)]

    loads = []
    for k, (src, dst) in enumerate(((t_hbm, tst), (u_hbm, ust))):
        for t in range(LT):
            loads.append(pltpu.make_async_copy(src.at[:, tile(t)], dst.at[t], in_sem.at[k * LT + t]))
    for copy in loads:
        copy.start()
    smalls_vmem = (obs_ref, noise_ref, var_ref, cells, pair_cells, pair_probes, probe_taper)
    smalls = [pltpu.make_async_copy(a, b, small_sem.at[i]) for i, (a, b) in enumerate(zip(smalls_hbm, smalls_vmem))]
    for copy in smalls:
        copy.start()

    bar = pltpu.get_barrier_semaphore()
    for d in range(1, NYR):
        pl.semaphore_signal(bar, 1, device_id=(s, ens_of(g, (y + d) % NYR)), device_id_type=MESH)
    for gg in sub_g:
        pl.semaphore_signal(bar, 1, device_id=(s, ens_of(gg, y)), device_id_type=MESH)

    @pl.when(has_up)
    def _():
        for gg in range(G):
            pl.semaphore_signal(bar, 1, device_id=(s_up, ens_of(gg, y)), device_id_type=MESH)

    @pl.when(has_dn)
    def _():
        for gg in range(G):
            pl.semaphore_signal(bar, 1, device_id=(s_dn, ens_of(gg, y)), device_id_type=MESH)

    lane = lax.broadcasted_iota(jnp.int32, (MEM, BLK), 1)
    low = lane < NZ
    height = lane % NZ
    top = height == NZ - 1
    wall = (height == 0) | top

    def bring(p):
        for t in range(LT):
            rows = pl.ds(p, MEM, PLANES)
            th[p * LT + t] = tst[t, rows, :]
            u0[p, :, tile(t)] = ust[t, rows, :]

    def viscosity(p):
        for t in range(LT):
            vv[p, :, tile(t)] = jnp.exp(th[p * LT + t])

    def loop(lo, hi, fn):
        def body(p, carry):
            fn(p)
            return carry

        lax.fori_loop(lo, hi, body, 0)

    def coefficients(p):
        def load(t):
            v = vv[p, :, tile(t % LT)]
            return v, pltpu.roll(v, NZ, 1)

        here = load(0)
        for t in range(LT):
            beside = load(t + 1)
            v = here[0]
            cy[p, :, tile(t)] = COEF * (v + jnp.where(low, here[1], beside[1]))
            cz[p, :, tile(t)] = jnp.where(top, 0.0, COEF * (v + pltpu.roll(v, BLK - 1, 1)))
            cd[p, :, tile(t)] = 1.0 - jnp.where(wall, COEF * (v + 1.0), 0.0)
            here = beside

    def face(p):
        for t in range(LT):
            cx[p, :, tile(t)] = COEF * (vv[p - 1, :, tile(t)] + vv[p, :, tile(t)])

    def step(src, off, p, lower, upper, emit):
        def load(t):
            v = src[p + off, :, tile(t % LT)]
            return v, pltpu.roll(v, NZ, 1)

        def flux_y(t, here, beside):
            f = cy[p, :, tile(t)] * (jnp.where(low, here[1], beside[1]) - here[0])
            return f, pltpu.roll(f, NZ, 1)

        here = first_one = load(0)
        before = last = load(LT - 1)
        f_prev = f_last = flux_y(LT - 1, last, first_one)
        for t in range(LT):
            beside = load(t + 1)
            f = flux_y(t, here, beside) if t < LT - 1 else f_last
            v = here[0]
            fz = cz[p, :, tile(t)] * (pltpu.roll(v, BLK - 1, 1) - v)
            new = cd[p, :, tile(t)] * v + ((f[0] - jnp.where(low, f_prev[1], f[1])) + (fz - pltpu.roll(fz, 1, 1)))
            if upper:
                new = new + cx[p + 1, :, tile(t)] * (src[p + 1 + off, :, tile(t)] - v)
            if lower:
                new = new - cx[p, :, tile(t)] * (v - src[p - 1 + off, :, tile(t)])
            emit(t, new)
            here, f_prev = beside, f

    def into(ref, *where):
        def emit(t, value):
            ref[(*where, slice(None), tile(t))] = value

        return emit

    for copy in loads:
        copy.wait()

    for p in (0, PLANES - 1):
        bring(p)

    pl.semaphore_wait(bar, NYR - 1 + G - 1 + G * has_up.astype(jnp.int32) + G * has_dn.astype(jnp.int32))

    ends = ((0, PLANES - 1, s_up, has_up), (1, 0, s_dn, has_dn))
    halo_field = [
        [
            remote(th.at[pl.ds(p * LT, LT)], thh.at[d], halo_s.at[d * 3], halo_r.at[d * 3], dest, e),
            remote(u0.at[p], uh.at[d], halo_s.at[d * 3 + 1], halo_r.at[d * 3 + 1], dest, e),
        ]
        for d, p, dest, _ in ends
    ]
    halo_part = [
        remote(ps.at[d], pr.at[d], halo_s.at[d * 3 + 2], halo_r.at[d * 3 + 2], dest, e) for d, p, dest, _ in ends
    ]
    for d, p, dest, has in ends:

        @pl.when(has)
        def _(d=d):
            for copy in halo_field[d]:
                copy.start()

    for p in (1, PLANES - 2):
        bring(p)
    for p in (0, 1, PLANES - 2, PLANES - 1):
        viscosity(p)
    for p in (0, PLANES - 1):
        coefficients(p)
    face(1)
    face(PLANES - 1)
    step(u0, 0, PLANES - 1, True, False, into(ps, 0))
    step(u0, 0, 0, False, True, into(ps, 1))
    for d, p, dest, has in ends:

        @pl.when(has)
        def _(d=d):
            halo_part[d].start()

    def pick(k, carry):
        upd[k] = th[pair_cells[0, k]]
        return carry

    loop(2, PLANES - 2, bring)
    for copy in smalls:
        copy.wait()
    lax.fori_loop(0, SLOTS, pick, 0, unroll=4)
    sub_copies = []
    for d, gg in enumerate(sub_g):
        sub_copies.append(
            remote(upd.at[pl.ds(gg * SPG, SPG)], thg.at[:, y, g], sub_s.at[d], sub_r.at[d], s, ens_of(gg, y))
        )
    for copy in sub_copies:
        copy.start()
    for i in range(SPG):
        thg[i, y, g] = upd[g * SPG + i]

    right, left = ens_of(g, (y + 1) % NYR), ens_of(g, (y + NYR - 1) % NYR)
    half = SPG // 2

    def ring(n):
        a, b = (y + NYR - n) % NYR, (y + n) % NYR
        if n < 3:
            src_r, src_l = thg.at[:, a], thg.at[:, b]
        else:
            src_r, src_l = thg.at[pl.ds(0, half), a], thg.at[pl.ds(half, half), b]
        return [
            remote(src_r, src_r, ring_s.at[n * 2], ring_r.at[n * 2], s, right),
            remote(src_l, src_l, ring_s.at[n * 2 + 1], ring_r.at[n * 2 + 1], s, left),
        ]

    rings = [ring(n) for n in range(4)]

    loop(2, PLANES - 2, viscosity)
    for copy in sub_copies:
        copy.wait_recv()
    for copy in rings[0]:
        copy.start()
    loop(1, PLANES - 1, coefficients)
    loop(2, PLANES - 1, face)

    def first(p):
        step(u0, 0, p, True, True, into(u1, p + 1))

    def second(p):
        def emit(t, value):
            u2[p * LT + t] = value

        step(u1, 1, p, True, True, emit)

    loop(1, PLANES - 1, first)
    loop(2, PLANES - 2, second)
    for copy in rings[0]:
        copy.wait_recv()
    for copy in rings[1]:
        copy.start()

    for d, p, dest, has in ends:

        @pl.when(jnp.logical_not((has_dn, has_up)[d]))
        def _(d=d):
            uh[d] = jnp.zeros_like(uh[d])
            thh[d] = jnp.zeros_like(thh[d])
            pr[d] = jnp.zeros_like(pr[d])

    for d, p, dest, has in ends:

        @pl.when((has_dn, has_up)[d])
        def _(d=d):
            for copy in halo_field[d]:
                copy.wait_recv()
            halo_part[d].wait_recv()

    keep_dn = has_dn.astype(F32)
    keep_up = has_up.astype(F32)
    for t in range(LT):
        w = (slice(None), tile(t))
        face_lo = COEF * (jnp.exp(thh[0, t]) + vv[(0, *w)])
        flux = face_lo * (u0[(0, *w)] - uh[(0, *w)])
        cx[(0, *w)] = face_lo
        u1[(0, *w)] = (pr[(0, *w)] + flux) * keep_dn
        u1[(1, *w)] = ps[(1, *w)] - flux
        face_hi = COEF * (jnp.exp(thh[1, t]) + vv[(PLANES - 1, *w)])
        flux = face_hi * (uh[(1, *w)] - u0[(PLANES - 1, *w)])
        cx[(PLANES, *w)] = face_hi
        u1[(PLANES + 1, *w)] = (pr[(1, *w)] - flux) * keep_up
        u1[(PLANES, *w)] = ps[(0, *w)] + flux
    loop(0, 2, second)
    loop(PLANES - 2, PLANES, second)

    def probe(i, accs):
        new = []
        for b in range(2):
            cell = cells[b * BLK + i]
            row = u2[cell >> 7]
            one = jnp.sum(jnp.where(lane == (cell & (BLK - 1)), row, 0.0), axis=1, keepdims=True)
            new.append(jnp.where(lane == i, one, accs[b]))
        return tuple(new)

    zero = jnp.zeros((MEM, BLK), F32)
    pred = lax.fori_loop(0, BLK, probe, (zero, zero), unroll=16)
    for b in range(2):
        agb[g, y, :, tile(b)] = pred[b]

    def onward(i, yy):
        return [
            remote(agb.at[g, yy], agb.at[g, yy], ag2_s.at[d * NYR + i], ag2_r.at[d * NYR + i], s, ens_of(gg, y))
            for d, gg in enumerate(sub_g)
        ]

    order = [4, 3, 5, 2, 6, 1, 7]
    ag1 = {
        d: remote(agb.at[g, y], agb.at[g, y], ag1_s.at[d - 1], ag1_r.at[d - 1], s, ens_of(g, (y + d) % NYR))
        for d in order
    }
    for d in order:
        ag1[d].start()
    scaled = [
        (obs_ref[:, tile(b)] + noise_ref[:, tile(b)] - pred[b]) / var_ref[:, tile(b)] for b in range(2)
    ]
    for b in range(2):
        scw[g, :, tile(b)] = scaled[b]
    sc = [
        remote(scw.at[g], scw.at[g], sc_s.at[d], sc_r.at[d], s, ens_of(gg, y)) for d, gg in enumerate(sub_g)
    ]
    for copy in sc:
        copy.start()
    ag2 = onward(0, y)
    for copy in ag2:
        copy.start()

    def back(p):
        for t in range(LT):
            ost[t, pl.ds(p, MEM, PLANES), :] = u2[p * LT + t]

    loop(0, PLANES, back)
    for copy in rings[1]:
        copy.wait_recv()
    for d in reversed(order):
        ag1[d].wait_recv()
        more = onward(d, (y + NYR - d) % NYR)
        for copy in more:
            copy.start()
        ag2 = ag2 + more
    for copy in rings[2]:
        copy.start()
    for copy in sc:
        copy.wait_recv()

    own_class = agb[g].reshape(NYR * MEM, 2 * BLK)
    wide = scw[...].reshape(G * MEM, 2 * BLK)
    half_a = [dot(wide[:, tile(b)], own_class[:, tile(b)], NT) for b in range(2)]
    a_part[...] = jnp.concatenate(half_a, axis=1).reshape(G, MEM, BLK)
    a_win[1, g] = a_part[g]
    ax_up = [remote(a_part.at[gg], a_win.at[0, g], ax_s.at[gg], ax_r.at[g], s_up, ens_of(gg, y)) for gg in range(G)]
    ax_dn = [
        remote(a_part.at[gg], a_win.at[2, g], ax_s.at[G + gg], ax_r.at[G + g], s_dn, ens_of(gg, y)) for gg in range(G)
    ]
    ax_own = [
        remote(a_part.at[gg], a_win.at[1, g], ax_s.at[2 * G + d], ax_r.at[2 * G + d], s, ens_of(gg, y))
        for d, gg in enumerate(sub_g)
    ]

    @pl.when(has_up)
    def _():
        for copy in ax_up:
            copy.start()

    @pl.when(has_dn)
    def _():
        for copy in ax_dn:
            copy.start()

    for copy in ax_own:
        copy.start()
    for d, has in ((0, has_dn), (1, has_up)):

        @pl.when(jnp.logical_not(has))
        def _(d=d):
            a_win[2 * d] = jnp.zeros((G, MEM, BLK), F32)
            for b in range(2):
                k_win[4 * d + b] = jnp.zeros((G, MEM, ALL), F32)

    for copy in ag2:
        copy.wait_recv()
    everyone = agb[...].reshape(ALL, 2 * BLK)
    anom[...] = everyone - jnp.sum(everyone, axis=0, keepdims=True) * (1.0 / ALL)
    for copy in rings[2]:
        copy.wait_recv()
    for copy in rings[3]:
        copy.start()
    for copy in ax_own:
        copy.wait_recv()
    for base, has in ((0, has_dn), (G, has_up)):

        @pl.when(has)
        def _(base=base):
            for gg in range(G):
                remote(a_part.at[0], a_win.at[0, g], ax_s.at[0], ax_r.at[base + gg], s, ens_of(gg, y)).wait_recv()

    for b in range(2):
        mixed = []
        for gg in range(G):
            mix = None
            for n in range(3):
                level = jnp.where(low, probe_taper[0, b, 2 * n].astype(F32), probe_taper[0, b, 2 * n + 1].astype(F32))
                term = a_win[n, gg] * level
                mix = term if mix is None else mix + term
            mixed.append(mix + pltpu.roll(mix, NZ, 1))
        mix = jnp.concatenate([jnp.where(low, mixed[q], mixed[q + 1]) for q in range(0, G, 2)], axis=1)
        corr = dot(mix * (1.0 / 256.0 / (ALL - 1)), anom[:, tile(b)], NN)
        gain = scaled[b] - corr / var_ref[:, tile(b)]
        gain_out[:, tile(b)] = gain
        kk = dot(gain, anom[:, tile(b)], NT)
        k_own[b] = kk
        k_win[2 + b, g] = kk
    kx_up = [remote(k_own, k_win.at[pl.ds(0, 2), g], kx_s.at[gg], kx_r.at[g], s_up, ens_of(gg, y)) for gg in range(G)]
    kx_dn = [
        remote(k_own, k_win.at[pl.ds(4, 2), g], kx_s.at[G + gg], kx_r.at[G + g], s_dn, ens_of(gg, y))
        for gg in range(G)
    ]
    kx_own = [
        remote(k_own, k_win.at[pl.ds(2, 2), g], kx_s.at[2 * G + d], kx_r.at[2 * G + d], s, ens_of(gg, y))
        for d, gg in enumerate(sub_g)
    ]

    @pl.when(has_up)
    def _():
        for copy in kx_up:
            copy.start()

    @pl.when(has_dn)
    def _():
        for copy in kx_dn:
            copy.start()

    for copy in kx_own:
        copy.start()
    for copy in rings[3]:
        copy.wait_recv()
    for copy in kx_own:
        copy.wait_recv()
    for base, has in ((0, has_dn), (G, has_up)):

        @pl.when(has)
        def _(base=base):
            for gg in range(G):
                remote(
                    k_own, k_win.at[pl.ds(0, 2), g], kx_s.at[0], kx_r.at[base + gg], s, ens_of(gg, y)
                ).wait_recv()

    for i in range(SPG):
        k = g * SPG + i
        left_side = k_win[pair_probes[0, k]].reshape(G * MEM, ALL)
        fields = jnp.concatenate([thg[i, :, gg].reshape(NYR * MEM, BLK) for gg in range(G)], axis=0)
        us[i] = dot(left_side, fields, NN).reshape(G, MEM, BLK)
    for copy in sub_copies:
        copy.wait_send()
    ux = [
        remote(us.at[:, gg], upd_out.at[pl.ds(g * SPG, SPG)], ux_s.at[d], ux_r.at[d], s, ens_of(gg, y))
        for d, gg in enumerate(sub_g)
    ]
    for copy in ux:
        copy.start()
    for i in range(SPG):
        upd_out[g * SPG + i] = us[i, g]

    for d, p, dest, has in ends:

        @pl.when(has)
        def _(d=d):
            for copy in halo_field[d]:
                copy.wait_send()
            halo_part[d].wait_send()
            for copy in (ax_up, ax_dn)[d] + (kx_up, kx_dn)[d]:
                copy.wait_send()

    for copy in [q for each in rings for q in each] + list(ag1.values()) + ag2 + sc + ax_own + kx_own:
        copy.wait_send()
    for copy in ux:
        copy.wait()


def tail_kernel(
    cells_hbm, taper_hbm, pair_counts, prior_st, theta_st, upd, gain_in, prior_out, post_out, gain_out, post_st,
    pair_cells, pair_taper, sem_i, sem_p, sem_o,
):
    smalls = [
        pltpu.make_async_copy(a, b, sem_i.at[i])
        for i, (a, b) in enumerate(((cells_hbm, pair_cells), (taper_hbm, pair_taper)))
    ]
    for copy in smalls:
        copy.start()
    stores = [pltpu.make_async_copy(prior_st.at[t], prior_out.at[:, tile(t)], sem_p.at[t]) for t in range(LT)]
    for copy in stores:
        copy.start()
    gain_out[...] = gain_in[...]
    for copy in smalls:
        copy.wait()

    def add(k, carry):
        b = pair_cells[0, k]
        w = jnp.where(k < pair_counts[0], pair_taper[0, k].astype(F32) * (1.0 / 256.0), 0.0) * (1.0 / (ALL - 1))
        rows = pl.ds(b // LT, MEM, PLANES)
        post_st[b % LT, rows, :] = post_st[b % LT, rows, :] + w * upd[k]
        return carry

    lax.fori_loop(0, SLOTS, add, 0)
    late = [pltpu.make_async_copy(post_st.at[t], post_out.at[:, tile(t)], sem_o.at[t]) for t in range(LT)]
    for copy in late:
        copy.start()
    for copy in stores + late:
        copy.wait()


def shards(u, theta, observed, obs_noise, obs_var, probe_cells, pair_cells, pair_probes, pair_taper, pair_counts, probe_taper):
    shape = u.shape
    rows, cols = shape[0] * shape[1], shape[2]
    u, theta = u.reshape(rows, cols), theta.reshape(rows, cols)
    hbm = pl.BlockSpec(memory_space=pltpu.HBM)
    vmem = pl.BlockSpec(memory_space=pltpu.VMEM)
    big = (PLANES, MEM, cols)
    staged = (LT, rows, BLK)
    flat = (PLANES * LT, MEM, BLK)
    dma = pltpu.SemaphoreType.DMA

    def buf(*dims):
        return pltpu.VMEM(dims, F32)

    def stay(x):
        return pltpu.with_memory_space_constraint(x, pltpu.HBM)

    def ints(*dims):
        return pltpu.SMEM(dims, jnp.int32)

    def arr(*dims):
        return jax.ShapeDtypeStruct(dims, F32)

    prior_st, theta_st, gain, upd = pl.pallas_call(
        main_kernel,
        name="assimilate",
        out_shape=(arr(*staged), arr(*staged), arr(MEM, 2 * BLK), arr(SLOTS, MEM, BLK)),
        in_specs=[hbm] * 9,
        out_specs=(vmem,) * 4,
        scratch_shapes=[
            buf(*staged), buf(*big), buf(*flat), buf(*big),
            buf(PLANES + 1, MEM, cols), buf(*big), buf(*big), buf(*big),
            buf(2, MEM, cols), buf(2, LT, MEM, BLK), buf(2, MEM, cols), buf(2, MEM, cols),
            buf(PLANES + 2, MEM, cols), buf(*flat),
            buf(SPG, NYR, G, MEM, BLK), buf(G, NYR, MEM, 2 * BLK), buf(G, MEM, 2 * BLK), buf(ALL, 2 * BLK),
            buf(G, MEM, BLK), buf(3, G, MEM, BLK), buf(2, MEM, ALL), buf(6, G, MEM, ALL),
            buf(SPG, G, MEM, BLK), buf(SLOTS, MEM, BLK),
            buf(1, 2 * BLK), buf(MEM, 2 * BLK), buf(1, 2 * BLK),
            ints(2 * BLK), ints(1, SLOTS), ints(1, SLOTS), ints(1, 2, 6),
            dma((2 * LT,)), dma((7,)), dma((6,)), dma((6,)), dma((3,)), dma((3,)), dma((8,)), dma((8,)),
            dma((7,)), dma((7,)), dma((24,)), dma((24,)), dma((3,)), dma((3,)),
            dma((11,)), dma((11,)), dma((11,)), dma((11,)), dma((3,)), dma((3,)),
        ],
        compiler_params=pltpu.CompilerParams(
            collective_id=0, has_side_effects=True, vmem_limit_bytes=28 * 1024 * 1024
        ),
    )(
        *map(
            stay,
            (
                u, theta, observed.reshape(1, -1), obs_noise, obs_var.reshape(1, -1), probe_cells, pair_cells,
                pair_probes, probe_taper,
            ),
        )
    )
    prior, post, gain, _ = pl.pallas_call(
        tail_kernel,
        name="tail",
        out_shape=(arr(rows, cols), arr(rows, cols), arr(MEM, 2 * BLK), arr(*staged)),
        in_specs=[hbm, hbm, pl.BlockSpec(memory_space=pltpu.SMEM)] + [vmem] * 4,
        out_specs=(hbm, hbm, vmem, vmem),
        input_output_aliases={4: 3},
        scratch_shapes=[
            ints(1, SLOTS), ints(1, SLOTS), dma((2,)), dma((LT,)), dma((LT,)),
        ],
        compiler_params=pltpu.CompilerParams(vmem_limit_bytes=16 * 1024 * 1024),
    )(stay(pair_cells), stay(pair_taper), pair_counts, prior_st, theta_st, upd, gain)
    return prior.reshape(shape), post.reshape(shape), gain


def solution(mesh):
    return jax.shard_map(
        shards,
        mesh=mesh,
        in_specs=(
            P("ens", "space", None), P("ens", "space", None), P("space"), P("ens", "space"), P("space"), P("space"),
            P("space", None), P("space", None), P("space", None), P("space"), P("space", None, None),
        ),
        out_specs=(P("ens", "space", None), P("ens", "space", None), P("ens", "space")),
        check_vma=False,
    )
```

time: 60.2 us -> 54.6 us (0.907)
  the two profiles are of different devices: /device:TPU:197 before, /device:TPU:193 now
where the time goes in v2:
time: 54.6 us; the launch traced here: 54.3 us
  Pallas kernels  53 us (97%)
  between operations  1.29 us (2%)
    pallas_call x1, Pallas kernels, shards(): pl.pallas_call(main_kernel, name='assimilate', out_shape=(arr(*staged), a...  49.9 us
    pallas_call x1, Pallas kernels, shards(): pl.pallas_call(tail_kernel, name='tail', out_shape=(arr(rows, cols), arr(...  3.13 us

profile of v2, /device:TPU:193, one launch (start us, length us, event | category | flops | bytes accessed | tf_op | source)
XLA Modules:
  0.0 54.3 jit_solution(246160343827333750)
XLA Ops:
  1.3 49.9 %assimilate.1 = (f32[16,128,128]{2,1,0:T(8,128)S(1)}, f32[16,128,128]{2,1,0:T(8,128)S(1)}, f32[8,256]{1,0:T(8,128)S(1)}, f32[32,8,128]{2,1,0:T(8,128)S(1)}) custom-call(f32[128,2048]{1,0:T(8,128)} %bitcast.6, f32[128,2048]{1,0:T(8,128)} %bitcast.7, f32[1,256]{1,0:T(1,128)} %bitcast.8, f32[8,256]{1,0:T(8,128)} %refs_1_.1, f32[1,256]{1,0:T(1,128)} %bitcast.9, ...), custom_call_target="tpu_custom_call" | custom-call | tf_op jit(solution)/shard_map/assimilate/pallas_call | solution.py:560
  51.2 3.1 %tail.1 = (f32[128,2048]{1,0:T(8,128)}, f32[128,2048]{1,0:T(8,128)}, f32[8,256]{1,0:T(8,128)}, f32[16,128,128]{2,1,0:T(8,128)S(1)}) custom-call(s32[1,32]{1,0:T(1,128)} %cells_hbm.1, s32[1,32]{1,0:T(1,128)} %taper_hbm.1, s32[1]{0:T(128)S(6)} %copy.16.pair_counts, f32[16,128,128]{2,1,0:T(8,128)S(1)} %get-tuple-element.10.prior_st, ...), custom_call_target="tpu_custom_call", output_to_operand_aliasing={{3}: (4, {})} | custom-call | tf_op jit(solution)/shard_map/tail/pallas_call | solution.py:592

commit v3 on v2

--- a/solution.py
+++ b/solution.py
@@ -110,22 +110,24 @@
     top = height == NZ - 1
     wall = (height == 0) | top
 
-    def bring(p):
-        for t in range(LT):
-            rows = pl.ds(p, MEM, PLANES)
-            th[p * LT + t] = tst[t, rows, :]
-            u0[p, :, tile(t)] = ust[t, rows, :]
+    def bring_theta(p):
+        for t in range(LT):
+            th[p * LT + t] = tst[t, pl.ds(p, MEM, PLANES), :]
+
+    def bring_u(p):
+        for t in range(LT):
+            u0[p, :, tile(t)] = ust[t, pl.ds(p, MEM, PLANES), :]
 
     def viscosity(p):
         for t in range(LT):
             vv[p, :, tile(t)] = jnp.exp(th[p * LT + t])
 
-    def loop(lo, hi, fn):
+    def loop(lo, hi, fn, unroll=2):
         def body(p, carry):
             fn(p)
             return carry
 
-        lax.fori_loop(lo, hi, body, 0)
+        lax.fori_loop(lo, hi, body, 0, unroll=unroll)
 
     def coefficients(p):
         def load(t):
@@ -176,75 +178,63 @@
 
         return emit
 
-    for copy in loads:
+    for copy in loads[:LT] + smalls:
         copy.wait()
-
-    for p in (0, PLANES - 1):
-        bring(p)
-
-    pl.semaphore_wait(bar, NYR - 1 + G - 1 + G * has_up.astype(jnp.int32) + G * has_dn.astype(jnp.int32))
-
-    ends = ((0, PLANES - 1, s_up, has_up), (1, 0, s_dn, has_dn))
-    halo_field = [
-        [
-            remote(th.at[pl.ds(p * LT, LT)], thh.at[d], halo_s.at[d * 3], halo_r.at[d * 3], dest, e),
-            remote(u0.at[p], uh.at[d], halo_s.at[d * 3 + 1], halo_r.at[d * 3 + 1], dest, e),
-        ]
-        for d, p, dest, _ in ends
-    ]
-    halo_part = [
-        remote(ps.at[d], pr.at[d], halo_s.at[d * 3 + 2], halo_r.at[d * 3 + 2], dest, e) for d, p, dest, _ in ends
-    ]
-    for d, p, dest, has in ends:
-
-        @pl.when(has)
-        def _(d=d):
-            for copy in halo_field[d]:
-                copy.start()
-
-    for p in (1, PLANES - 2):
-        bring(p)
-    for p in (0, 1, PLANES - 2, PLANES - 1):
+    loop(0, PLANES, bring_theta)
+
+    def pick(k, carry):
+        upd[k] = th[pair_cells[0, k]]
+        return carry
+
+    lax.fori_loop(0, SLOTS, pick, 0, unroll=4)
+    thg[y, g] = upd[pl.ds(g * SPG, SPG)]
+    sub_copies = [
+        remote(upd.at[pl.ds(gg * SPG, SPG)], thg.at[y, g], sub_s.at[d], sub_r.at[d], s, ens_of(gg, y))
+        for d, gg in enumerate(sub_g)
+    ]
+
+    rim = (0, 1, PLANES - 2, PLANES - 1)
+    for p in rim:
         viscosity(p)
     for p in (0, PLANES - 1):
         coefficients(p)
     face(1)
     face(PLANES - 1)
+    for copy in loads[LT:]:
+        copy.wait()
+    for p in rim:
+        bring_u(p)
     step(u0, 0, PLANES - 1, True, False, into(ps, 0))
     step(u0, 0, 0, False, True, into(ps, 1))
+
+    ends = ((0, PLANES - 1, s_up, has_up), (1, 0, s_dn, has_dn))
+    halo = [
+        [
+            remote(th.at[pl.ds(p * LT, LT)], thh.at[d], halo_s.at[d * 3], halo_r.at[d * 3], dest, e),
+            remote(u0.at[p], uh.at[d], halo_s.at[d * 3 + 1], halo_r.at[d * 3 + 1], dest, e),
+            remote(ps.at[d], pr.at[d], halo_s.at[d * 3 + 2], halo_r.at[d * 3 + 2], dest, e),
+        ]
+        for d, p, dest, _ in ends
+    ]
+    pl.semaphore_wait(bar, NYR - 1 + G - 1 + G * has_up.astype(jnp.int32) + G * has_dn.astype(jnp.int32))
+    for copy in sub_copies:
+        copy.start()
     for d, p, dest, has in ends:
 
         @pl.when(has)
         def _(d=d):
-            halo_part[d].start()
-
-    def pick(k, carry):
-        upd[k] = th[pair_cells[0, k]]
-        return carry
-
-    loop(2, PLANES - 2, bring)
-    for copy in smalls:
-        copy.wait()
-    lax.fori_loop(0, SLOTS, pick, 0, unroll=4)
-    sub_copies = []
-    for d, gg in enumerate(sub_g):
-        sub_copies.append(
-            remote(upd.at[pl.ds(gg * SPG, SPG)], thg.at[:, y, g], sub_s.at[d], sub_r.at[d], s, ens_of(gg, y))
-        )
-    for copy in sub_copies:
-        copy.start()
-    for i in range(SPG):
-        thg[i, y, g] = upd[g * SPG + i]
+            for copy in halo[d]:
+                copy.start()
 
     right, left = ens_of(g, (y + 1) % NYR), ens_of(g, (y + NYR - 1) % NYR)
-    half = SPG // 2
+    half = G // 2
 
     def ring(n):
         a, b = (y + NYR - n) % NYR, (y + n) % NYR
         if n < 3:
-            src_r, src_l = thg.at[:, a], thg.at[:, b]
+            src_r, src_l = thg.at[a], thg.at[b]
         else:
-            src_r, src_l = thg.at[pl.ds(0, half), a], thg.at[pl.ds(half, half), b]
+            src_r, src_l = thg.at[a, pl.ds(0, half)], thg.at[b, pl.ds(half, half)]
         return [
             remote(src_r, src_r, ring_s.at[n * 2], ring_r.at[n * 2], s, right),
             remote(src_l, src_l, ring_s.at[n * 2 + 1], ring_r.at[n * 2 + 1], s, left),
@@ -253,12 +243,9 @@
     rings = [ring(n) for n in range(4)]
 
     loop(2, PLANES - 2, viscosity)
-    for copy in sub_copies:
-        copy.wait_recv()
-    for copy in rings[0]:
-        copy.start()
+    loop(2, PLANES - 2, bring_u)
     loop(1, PLANES - 1, coefficients)
-    loop(2, PLANES - 1, face)
+    loop(2, PLANES - 1, face, 1)
 
     def first(p):
         step(u0, 0, p, True, True, into(u1, p + 1))
@@ -270,11 +257,11 @@
         step(u1, 1, p, True, True, emit)
 
     loop(1, PLANES - 1, first)
+    for copy in sub_copies:
+        copy.wait_recv()
+    for copy in rings[0]:
+        copy.start()
     loop(2, PLANES - 2, second)
-    for copy in rings[0]:
-        copy.wait_recv()
-    for copy in rings[1]:
-        copy.start()
 
     for d, p, dest, has in ends:
 
@@ -288,9 +275,8 @@
 
         @pl.when((has_dn, has_up)[d])
         def _(d=d):
-            for copy in halo_field[d]:
+            for copy in halo[d]:
                 copy.wait_recv()
-            halo_part[d].wait_recv()
 
     keep_dn = has_dn.astype(F32)
     keep_up = has_up.astype(F32)
@@ -309,6 +295,11 @@
     loop(0, 2, second)
     loop(PLANES - 2, PLANES, second)
 
+    for copy in rings[0]:
+        copy.wait_recv()
+    for copy in rings[1]:
+        copy.start()
+
     def probe(i, accs):
         new = []
         for b in range(2):
@@ -355,14 +346,14 @@
             ost[t, pl.ds(p, MEM, PLANES), :] = u2[p * LT + t]
 
     loop(0, PLANES, back)
-    for copy in rings[1]:
-        copy.wait_recv()
     for d in reversed(order):
         ag1[d].wait_recv()
         more = onward(d, (y + NYR - d) % NYR)
         for copy in more:
             copy.start()
         ag2 = ag2 + more
+    for copy in rings[1]:
+        copy.wait_recv()
     for copy in rings[2]:
         copy.start()
     for copy in sc:
@@ -399,8 +390,7 @@
         @pl.when(jnp.logical_not(has))
         def _(d=d):
             a_win[2 * d] = jnp.zeros((G, MEM, BLK), F32)
-            for b in range(2):
-                k_win[4 * d + b] = jnp.zeros((G, MEM, ALL), F32)
+            k_win[pl.ds(2 * d * G * 2, G * 2)] = jnp.zeros((G * 2, MEM, ALL), F32)
 
     for copy in ag2:
         copy.wait_recv()
@@ -434,14 +424,14 @@
         gain_out[:, tile(b)] = gain
         kk = dot(gain, anom[:, tile(b)], NT)
         k_own[b] = kk
-        k_win[2 + b, g] = kk
-    kx_up = [remote(k_own, k_win.at[pl.ds(0, 2), g], kx_s.at[gg], kx_r.at[g], s_up, ens_of(gg, y)) for gg in range(G)]
+        k_win[(G + g) * 2 + b] = kk
+    kx_up = [remote(k_own, k_win.at[pl.ds(g * 2, 2)], kx_s.at[gg], kx_r.at[g], s_up, ens_of(gg, y)) for gg in range(G)]
     kx_dn = [
-        remote(k_own, k_win.at[pl.ds(4, 2), g], kx_s.at[G + gg], kx_r.at[G + g], s_dn, ens_of(gg, y))
+        remote(k_own, k_win.at[pl.ds((2 * G + g) * 2, 2)], kx_s.at[G + gg], kx_r.at[G + g], s_dn, ens_of(gg, y))
         for gg in range(G)
     ]
     kx_own = [
-        remote(k_own, k_win.at[pl.ds(2, 2), g], kx_s.at[2 * G + d], kx_r.at[2 * G + d], s, ens_of(gg, y))
+        remote(k_own, k_win.at[pl.ds((G + g) * 2, 2)], kx_s.at[2 * G + d], kx_r.at[2 * G + d], s, ens_of(gg, y))
         for d, gg in enumerate(sub_g)
     ]
 
@@ -467,32 +457,33 @@
         def _(base=base):
             for gg in range(G):
                 remote(
-                    k_own, k_win.at[pl.ds(0, 2), g], kx_s.at[0], kx_r.at[base + gg], s, ens_of(gg, y)
+                    k_own, k_win.at[pl.ds(g * 2, 2)], kx_s.at[0], kx_r.at[base + gg], s, ens_of(gg, y)
                 ).wait_recv()
 
     for i in range(SPG):
         k = g * SPG + i
-        left_side = k_win[pair_probes[0, k]].reshape(G * MEM, ALL)
-        fields = jnp.concatenate([thg[i, :, gg].reshape(NYR * MEM, BLK) for gg in range(G)], axis=0)
-        us[i] = dot(left_side, fields, NN).reshape(G, MEM, BLK)
+        j = pair_probes[0, k]
+        at = (j >> 1) * (2 * G) + (j & 1)
+        left_side = jnp.concatenate([k_win[at + 2 * gg] for gg in range(G)], axis=0)
+        fields = jnp.concatenate([thg[yy, gg, i] for gg in range(G) for yy in range(NYR)], axis=0)
+        us[:, i] = dot(left_side, fields, NN).reshape(G, MEM, BLK)
     for copy in sub_copies:
         copy.wait_send()
     ux = [
-        remote(us.at[:, gg], upd_out.at[pl.ds(g * SPG, SPG)], ux_s.at[d], ux_r.at[d], s, ens_of(gg, y))
+        remote(us.at[gg], upd_out.at[pl.ds(g * SPG, SPG)], ux_s.at[d], ux_r.at[d], s, ens_of(gg, y))
         for d, gg in enumerate(sub_g)
     ]
     for copy in ux:
         copy.start()
     for i in range(SPG):
-        upd_out[g * SPG + i] = us[i, g]
+        upd_out[g * SPG + i] = us[g, i]
 
     for d, p, dest, has in ends:
 
         @pl.when(has)
         def _(d=d):
-            for copy in halo_field[d]:
+            for copy in halo[d]:
                 copy.wait_send()
-            halo_part[d].wait_send()
             for copy in (ax_up, ax_dn)[d] + (kx_up, kx_dn)[d]:
                 copy.wait_send()
 
@@ -568,9 +559,9 @@
             buf(PLANES + 1, MEM, cols), buf(*big), buf(*big), buf(*big),
             buf(2, MEM, cols), buf(2, LT, MEM, BLK), buf(2, MEM, cols), buf(2, MEM, cols),
             buf(PLANES + 2, MEM, cols), buf(*flat),
-            buf(SPG, NYR, G, MEM, BLK), buf(G, NYR, MEM, 2 * BLK), buf(G, MEM, 2 * BLK), buf(ALL, 2 * BLK),
-            buf(G, MEM, BLK), buf(3, G, MEM, BLK), buf(2, MEM, ALL), buf(6, G, MEM, ALL),
-            buf(SPG, G, MEM, BLK), buf(SLOTS, MEM, BLK),
+            buf(NYR, G, SPG, MEM, BLK), buf(G, NYR, MEM, 2 * BLK), buf(G, MEM, 2 * BLK), buf(ALL, 2 * BLK),
+            buf(G, MEM, BLK), buf(3, G, MEM, BLK), buf(2, MEM, ALL), buf(3 * G * 2, MEM, ALL),
+            buf(G, SPG, MEM, BLK), buf(SLOTS, MEM, BLK),
             buf(1, 2 * BLK), buf(MEM, 2 * BLK), buf(1, 2 * BLK),
             ints(2 * BLK), ints(1, SLOTS), ints(1, SLOTS), ints(1, 2, 6),
             dma((2 * LT,)), dma((7,)), dma((6,)), dma((6,)), dma((3,)), dma((3,)), dma((8,)), dma((8,)),

time: 54.6 us -> 49.4 us (0.905)
  the two profiles are of different devices: /device:TPU:193 before, /device:TPU:197 now
where the time goes in v3:
time: 49.4 us; the launch traced here: 49.2 us
  Pallas kernels  47.9 us (97%)
  between operations  1.29 us (3%)
    pallas_call x1, Pallas kernels, shards(): pl.pallas_call(main_kernel, name='assimilate', out_shape=(arr(*staged), a...  44.7 us
    pallas_call x1, Pallas kernels, shards(): pl.pallas_call(tail_kernel, name='tail', out_shape=(arr(rows, cols), arr(...  3.13 us

profile of v3, /device:TPU:197, one launch (start us, length us, event | category | flops | bytes accessed | tf_op | source)
XLA Modules:
  0.0 49.2 jit_solution(14069402110813240230)
XLA Ops:
  1.3 44.7 %assimilate.1 = (f32[16,128,128]{2,1,0:T(8,128)S(1)}, f32[16,128,128]{2,1,0:T(8,128)S(1)}, f32[8,256]{1,0:T(8,128)S(1)}, f32[32,8,128]{2,1,0:T(8,128)S(1)}) custom-call(f32[128,2048]{1,0:T(8,128)} %bitcast.6, f32[128,2048]{1,0:T(8,128)} %bitcast.7, f32[1,256]{1,0:T(1,128)} %bitcast.8, f32[8,256]{1,0:T(8,128)} %refs_1_.1, f32[1,256]{1,0:T(1,128)} %bitcast.9, ...), custom_call_target="tpu_custom_call" | custom-call | tf_op jit(solution)/shard_map/assimilate/pallas_call | solution.py:551
  46.0 3.1 %tail.1 = (f32[128,2048]{1,0:T(8,128)}, f32[128,2048]{1,0:T(8,128)}, f32[8,256]{1,0:T(8,128)}, f32[16,128,128]{2,1,0:T(8,128)S(1)}) custom-call(s32[1,32]{1,0:T(1,128)} %cells_hbm.1, s32[1,32]{1,0:T(1,128)} %taper_hbm.1, s32[1]{0:T(128)S(6)} %copy.16.pair_counts, f32[16,128,128]{2,1,0:T(8,128)S(1)} %get-tuple-element.10.prior_st, ...), custom_call_target="tpu_custom_call", output_to_operand_aliasing={{3}: (4, {})} | custom-call | tf_op jit(solution)/shard_map/tail/pallas_call | solution.py:583

commit v4 on v3

--- a/solution.py
+++ b/solution.py
@@ -263,6 +263,11 @@
         copy.start()
     loop(2, PLANES - 2, second)
 
+    for copy in rings[0]:
+        copy.wait_recv()
+    for copy in rings[1]:
+        copy.start()
+
     for d, p, dest, has in ends:
 
         @pl.when(jnp.logical_not((has_dn, has_up)[d]))
@@ -295,11 +300,6 @@
     loop(0, 2, second)
     loop(PLANES - 2, PLANES, second)
 
-    for copy in rings[0]:
-        copy.wait_recv()
-    for copy in rings[1]:
-        copy.start()
-
     def probe(i, accs):
         new = []
         for b in range(2):
@@ -348,14 +348,15 @@
     loop(0, PLANES, back)
     for d in reversed(order):
         ag1[d].wait_recv()
+        if d == 2:
+            for copy in rings[1]:
+                copy.wait_recv()
+            for copy in rings[2]:
+                copy.start()
         more = onward(d, (y + NYR - d) % NYR)
         for copy in more:
             copy.start()
         ag2 = ag2 + more
-    for copy in rings[1]:
-        copy.wait_recv()
-    for copy in rings[2]:
-        copy.start()
     for copy in sc:
         copy.wait_recv()
 
@@ -396,10 +397,6 @@
         copy.wait_recv()
     everyone = agb[...].reshape(ALL, 2 * BLK)
     anom[...] = everyone - jnp.sum(everyone, axis=0, keepdims=True) * (1.0 / ALL)
-    for copy in rings[2]:
-        copy.wait_recv()
-    for copy in rings[3]:
-        copy.start()
     for copy in ax_own:
         copy.wait_recv()
     for base, has in ((0, has_dn), (G, has_up)):
@@ -447,6 +444,10 @@
 
     for copy in kx_own:
         copy.start()
+    for copy in rings[2]:
+        copy.wait_recv()
+    for copy in rings[3]:
+        copy.start()
     for copy in rings[3]:
         copy.wait_recv()
     for copy in kx_own:
@@ -517,7 +518,7 @@
         post_st[b % LT, rows, :] = post_st[b % LT, rows, :] + w * upd[k]
         return carry
 
-    lax.fori_loop(0, SLOTS, add, 0)
+    lax.fori_loop(0, SLOTS, add, 0, unroll=8)
     late = [pltpu.make_async_copy(post_st.at[t], post_out.at[:, tile(t)], sem_o.at[t]) for t in range(LT)]
     for copy in late:
         copy.start()

time: 49.4 us -> 48.4 us (0.980)
  Pallas kernels: 47.9 us -> 46.9 us
    pallas_call x1, Pallas kernels: 44.7 us -> 44.1 us  [shards(): pl.pallas_call(main_kernel, name='assimilate', out_shape=(arr(*staged), a...]
where the time goes in v4:
time: 48.4 us; the launch traced here: 48.2 us
  Pallas kernels  46.9 us (97%)
  between operations  1.29 us (3%)
    pallas_call x1, Pallas kernels, shards(): pl.pallas_call(main_kernel, name='assimilate', out_shape=(arr(*staged), a...  44.1 us
    pallas_call x1, Pallas kernels, shards(): pl.pallas_call(tail_kernel, name='tail', out_shape=(arr(rows, cols), arr(...  2.86 us

profile of v4, /device:TPU:197, one launch (start us, length us, event | category | flops | bytes accessed | tf_op | source)
XLA Modules:
  0.0 48.2 jit_solution(12592451307595323287)
XLA Ops:
  1.3 44.1 %assimilate.1 = (f32[16,128,128]{2,1,0:T(8,128)S(1)}, f32[16,128,128]{2,1,0:T(8,128)S(1)}, f32[8,256]{1,0:T(8,128)S(1)}, f32[32,8,128]{2,1,0:T(8,128)S(1)}) custom-call(f32[128,2048]{1,0:T(8,128)} %bitcast.6, f32[128,2048]{1,0:T(8,128)} %bitcast.7, f32[1,256]{1,0:T(1,128)} %bitcast.8, f32[8,256]{1,0:T(8,128)} %refs_1_.1, f32[1,256]{1,0:T(1,128)} %bitcast.9, ...), custom_call_target="tpu_custom_call" | custom-call | tf_op jit(solution)/shard_map/assimilate/pallas_call | solution.py:552
  45.4 2.9 %tail.1 = (f32[128,2048]{1,0:T(8,128)}, f32[128,2048]{1,0:T(8,128)}, f32[8,256]{1,0:T(8,128)}, f32[16,128,128]{2,1,0:T(8,128)S(1)}) custom-call(s32[1,32]{1,0:T(1,128)} %cells_hbm.1, s32[1,32]{1,0:T(1,128)} %taper_hbm.1, s32[1]{0:T(128)S(6)} %copy.16.pair_counts, f32[16,128,128]{2,1,0:T(8,128)S(1)} %get-tuple-element.10.prior_st, ...), custom_call_target="tpu_custom_call", output_to_operand_aliasing={{3}: (4, {})} | custom-call | tf_op jit(solution)/shard_map/tail/pallas_call | solution.py:584

commit v5 on v4

--- a/solution.py
+++ b/solution.py
@@ -77,17 +77,6 @@
 
     sub_g = [(g + d) % G for d in range(1, G)]
 
-    loads = []
-    for k, (src, dst) in enumerate(((t_hbm, tst), (u_hbm, ust))):
-        for t in range(LT):
-            loads.append(pltpu.make_async_copy(src.at[:, tile(t)], dst.at[t], in_sem.at[k * LT + t]))
-    for copy in loads:
-        copy.start()
-    smalls_vmem = (obs_ref, noise_ref, var_ref, cells, pair_cells, pair_probes, probe_taper)
-    smalls = [pltpu.make_async_copy(a, b, small_sem.at[i]) for i, (a, b) in enumerate(zip(smalls_hbm, smalls_vmem))]
-    for copy in smalls:
-        copy.start()
-
     bar = pltpu.get_barrier_semaphore()
     for d in range(1, NYR):
         pl.semaphore_signal(bar, 1, device_id=(s, ens_of(g, (y + d) % NYR)), device_id_type=MESH)
@@ -103,6 +92,17 @@
     def _():
         for gg in range(G):
             pl.semaphore_signal(bar, 1, device_id=(s_dn, ens_of(gg, y)), device_id_type=MESH)
+
+    loads = []
+    for k, (src, dst) in enumerate(((t_hbm, tst), (u_hbm, ust))):
+        for t in range(LT):
+            loads.append(pltpu.make_async_copy(src.at[:, tile(t)], dst.at[t], in_sem.at[k * LT + t]))
+    for copy in loads:
+        copy.start()
+    smalls_vmem = (obs_ref, noise_ref, var_ref, cells, pair_cells, pair_probes, probe_taper)
+    smalls = [pltpu.make_async_copy(a, b, small_sem.at[i]) for i, (a, b) in enumerate(zip(smalls_hbm, smalls_vmem))]
+    for copy in smalls:
+        copy.start()
 
     lane = lax.broadcasted_iota(jnp.int32, (MEM, BLK), 1)
     low = lane < NZ

time: 48.4 us -> 48.4 us (level)
  no operation moved by 1% of the time
where the time goes in v5:
time: 48.4 us; the launch traced here: 48.2 us
  Pallas kernels  46.9 us (97%)
  between operations  1.29 us (3%)
    pallas_call x1, Pallas kernels, shards(): pl.pallas_call(main_kernel, name='assimilate', out_shape=(arr(*staged), a...  44 us
    pallas_call x1, Pallas kernels, shards(): pl.pallas_call(tail_kernel, name='tail', out_shape=(arr(rows, cols), arr(...  2.86 us

profile of v5, /device:TPU:197, one launch (start us, length us, event | category | flops | bytes accessed | tf_op | source)
XLA Modules:
  0.0 48.2 jit_solution(5984783234971871214)
XLA Ops:
  1.3 44.0 %assimilate.1 = (f32[16,128,128]{2,1,0:T(8,128)S(1)}, f32[16,128,128]{2,1,0:T(8,128)S(1)}, f32[8,256]{1,0:T(8,128)S(1)}, f32[32,8,128]{2,1,0:T(8,128)S(1)}) custom-call(f32[128,2048]{1,0:T(8,128)} %bitcast.6, f32[128,2048]{1,0:T(8,128)} %bitcast.7, f32[1,256]{1,0:T(1,128)} %bitcast.8, f32[8,256]{1,0:T(8,128)} %refs_1_.1, f32[1,256]{1,0:T(1,128)} %bitcast.9, ...), custom_call_target="tpu_custom_call" | custom-call | tf_op jit(solution)/shard_map/assimilate/pallas_call | solution.py:552
  45.3 2.9 %tail.1 = (f32[128,2048]{1,0:T(8,128)}, f32[128,2048]{1,0:T(8,128)}, f32[8,256]{1,0:T(8,128)}, f32[16,128,128]{2,1,0:T(8,128)S(1)}) custom-call(s32[1,32]{1,0:T(1,128)} %cells_hbm.1, s32[1,32]{1,0:T(1,128)} %taper_hbm.1, s32[1]{0:T(128)S(6)} %copy.16.pair_counts, f32[16,128,128]{2,1,0:T(8,128)S(1)} %get-tuple-element.10.prior_st, ...), custom_call_target="tpu_custom_call", output_to_operand_aliasing={{3}: (4, {})} | custom-call | tf_op jit(solution)/shard_map/tail/pallas_call | solution.py:584
